TPU v7x, 256 devices: a whole 4x4x8 slice. The times are simulated.
256 devices in a mesh: grid: 16 (over y, x), band: 8 (over z), pole: 2 (over core).
Axes of the slice: x: 4, y: 4, z: 8, core: 2. Of those that a mesh axis runs over, the one named last changes fastest.
Arguments:
- solution: bfloat16 [2, 512, 64, 16, 256], P('pole', 'band', 'grid'), may hold values from -6 to 6
- proj_vals: bfloat16 [256, 128, 2048], P('grid'), may hold values from -0.125 to 0.125
- slot_offset: int32 [256], P('grid'), may hold values from 0 to 14336
- slot_block: int32 [16, 16], replicated, may hold values from 0 to 127, as said below
- proj_coef: float32 [128, 128], P('grid'), may hold values from -0.015625 to 0.015625
- pole_weight: float32 [2], P('pole'), may hold values from 0.25 to 1
- proj_atom: int32 [128, 128], P('grid'), may hold values from -1 to 55, as said below
Outputs:
- forces: float32 [3, 896], P(None, 'grid')
Inputs may be any that keep to these rules, and one draw needn't show every extreme that they name: `slot_block`: the blocks of one brick's row differ; at most 2 of them belong to one owner (block // 8); in every draw one owner gets exactly 2 blocks from every brick. `proj_atom`: each block of owner o holds 18 projectors of each of 7 of o's atoms, each of o's atoms in exactly one block, and -1 in its other positions.
All inputs are finite; a program needn't handle non-finite values.
Results may differ from a plain program's by a relative error of at most 0.013.
Values may be sent and summed in bfloat16 or wider, within the bound.
No kernel may reach another device: no remote copies, remote signals or barrier semaphores. Data moves between devices by JAX's collectives and lax.ppermute only.
A program may use at most 128 MiB of HBM per device.

v0:
```python
import jax
import jax.numpy as jnp
from jax import lax
from jax.sharding import PartitionSpec as P

ATOM_OWN = 56


def padded(x, sides, width):
    for axis, dim in sides:
        peers, length = (lax.axis_size(axis), x.shape[dim])
        up = [(i, (i + 1) % peers) for i in range(peers)]
        down = [(j, i) for i, j in up]
        last = lax.slice_in_dim(x, length - width, length, axis=dim)
        initial = lax.slice_in_dim(x, 0, width, axis=dim)
        before = lax.ppermute(last, axis, up)
        after = lax.ppermute(initial, axis, down)
        x = jnp.concatenate([before, x, after], axis=dim)
    return x


def derivative(upper, lower):
    return ((upper.astype(jnp.float32) - lower.astype(jnp.float32)) * 0.5).astype(jnp.bfloat16)


def build_fields(extended):
    middle = extended[:, :, 1:-1]
    grad_x = derivative(extended[:, :, 2:], extended[:, :, :-2])
    grad_y = derivative(jnp.roll(middle, -1, axis=3), jnp.roll(middle, 1, axis=3))
    grad_z = derivative(jnp.roll(middle, -1, axis=4), jnp.roll(middle, 1, axis=4))
    stacked = jnp.stack([middle, grad_x, grad_y, grad_z], axis=0)
    return stacked.reshape(4 * middle.shape[0] * middle.shape[1], -1)


def slot_products(fields, projector, offsets):
    window_cells = projector.shape[2]

    def one_slot(pair):
        block_vals, offset = pair
        window = lax.dynamic_slice_in_dim(fields, offset, window_cells, 1)
        return lax.dot_general(
            window, block_vals, (((1,), (1,)), ((), ())), preferred_element_type=jnp.float32
        ).astype(jnp.bfloat16)

    return lax.map(one_slot, (projector, offsets))


def per_device(solution, proj_vals, slot_offset, slot_block, proj_coef, pole_weight, proj_atom):
    extended = padded(solution, (("grid", 2),), 1)
    fields = build_fields(extended)
    partials = slot_products(fields, proj_vals, slot_offset)
    slot_count, height, proj_width = partials.shape
    flat_parts = partials.reshape(slot_count, height * proj_width)
    bricks_all = lax.axis_size("grid")
    owned = proj_coef.shape[0]
    brick_index = lax.axis_index("grid")
    total_blocks = owned * bricks_all
    own_ids = lax.dynamic_index_in_dim(slot_block, brick_index, 0, keepdims=False)
    placing = (own_ids[None, :] == jnp.arange(total_blocks, dtype=jnp.int32)[:, None]).astype(
        jnp.bfloat16
    )
    dense = jnp.dot(placing, flat_parts, preferred_element_type=jnp.float32)
    coefficients = lax.psum_scatter(
        dense.reshape(total_blocks, height, proj_width).astype(jnp.bfloat16),
        "grid",
        scatter_dimension=0,
        tiled=True,
    ).astype(jnp.float32)
    pole_count = pole_weight.shape[0]
    shaped = coefficients.reshape(owned, 4, pole_count, -1, proj_width)
    weighted = jnp.einsum("bpci,bxpci,p->xbi", shaped[:, 0], shaped[:, 1:], pole_weight)
    force_terms = -2.0 * weighted * proj_coef[None]
    onehot = (proj_atom[:, :, None] == jnp.arange(ATOM_OWN, dtype=jnp.int32)).astype(jnp.float32)
    partial_forces = jnp.einsum("xbi,bia->xa", force_terms, onehot)
    return lax.psum(partial_forces, ("band", "pole"))


def solution(mesh):
    placed = (
        P("pole", "band", "grid", None, None),
        P("grid", None, None),
        P("grid"),
        P(),
        P("grid", None),
        P("pole"),
        P("grid", None),
    )
    return jax.shard_map(
        per_device, mesh=mesh, in_specs=placed, out_specs=P(None, "grid"), check_vma=False
    )
```

profile of v0, /device:TPU:1, one launch (start us, length us, event | category | flops | bytes accessed | tf_op | source)
XLA Modules:
  0.0 328.4 jit_solution(10868088315402862352)
XLA Ops:
  6.5 2.4 fusion.18
  9.0 5.7 %collective-permute-start = (bf16[1,64,1,16,256]{4,3,2,1,0:T(8,128)(2,1)}, bf16[1,64,1,16,256]{4,3,2,1,0:T(8,128)(2,1)}, u32[]{:S(2)}, u32[]{:S(2)}) collective-permute-start(bf16[1,64,1,16,256]{4,3,2,1,0:T(8,128)(2,1)} %get-tuple-element.43), channel_id=1, source_target_pairs={{16,0},{32,16},{48,32},{64,48},{80,64},{96,80},{112,96},{128,112},... | collective-permute-start | bytes 1572872 | tf_op jit(solution)/shard_map/ppermute | solution.py:17
  14.7 2.7 fusion.19
  17.4 2.7 slice_bitcast_fusion.2
  23.8 2.4 copy.42
  26.2 2.6 copy.26
  31.8 4.5 %multiply_convert_fusion.1 = bf16[1,1,64,4,16,256]{5,4,3,2,1,0:T(8,128)(2,1)S(1)} fusion(bf16[1,1,64,4,1,256]{5,4,3,2,1,0:T(2,128)(2,1)S(1)} %copy.22, bf16[1,1,64,4,15,256]{5,4,3,2,1,0:T(8,128)(2,1)} %get-tuple-element.48, bf16[1,1,64,4,15,256]{5,4,3,2,1,0:T(8,128)(2,1)} %get-tuple-element.47, bf16[1,1,64,4,1,256]{5,4,3,2,1,0:T(2,128)(2,1)} %copy.24), kind=kLoop, calls=%fused_computation.10 | loop fusion | flops 11534336 | bytes 6291456 | tf_op jit(solution)/shard_map/convert_element_type | solution.py:23
  37.6 2.3 multiply_convert_fusion
  39.9 2.1 fusion.6
  42.0 3.9 %pad_maximum_fusion = bf16[4,1,64,4,16,256]{5,4,3,2,1,0:T(8,128)(2,1)} fusion(bf16[1,1,64,4,16,256]{5,4,3,2,1,0:T(8,128)(2,1)S(1)} %multiply_convert_fusion, bf16[1,1,64,4,16,256]{5,4,3,2,1,0:T(8,128)(2,1)S(1)} %multiply_convert_fusion.1, bf16[1,1,64,4,16,256]{5,4,3,2,1,0:T(8,128)(2,1)S(1)} %fusion.6, bf16[1,1,64,4,16,256]{5,4,3,2,1,0:T(8,128)(2,1)S(1)} %bitcast.85), kind=kLoop, calls=%fused_computation.7 | loop fusion | flops 12582912 | bytes 16777216 | tf_op jit(solution)/shard_map/stack | solution.py:31
  45.9 13.6 %reshape.205 = bf16[256,16384]{1,0:T(8,128)(2,1)} reshape(bf16[4,1,64,4,16,256]{5,4,3,2,1,0:T(8,128)(2,1)} %pad_maximum_fusion) | data formatting | bytes 16777216 | tf_op jit(solution)/shard_map/reshape | solution.py:32
  59.5 75.4 %while.10 = (s32[]{:T(128)}, bf16[16,256,128]{2,1,0:T(8,128)(2,1)S(1)}, s32[16]{0:T(128)S(1)}, bf16[256,16384]{1,0:T(8,128)(2,1)}, bf16[16,128,2048]{2,1,0:T(8,128)(2,1)}, /*index=5*/s32[]{:T(128)}, s32[]{:T(128)}, s32[]{:T(128)}) while((s32[]{:T(128)}, bf16[16,256,128]{2,1,0:T(8,128)(2,1)S(1)}, s32[16]{0:T(128)S(1)}, ...), condition=%wide.region_1.2_spmd, body=%wide.region_0.1_spmd.sunk | while | flops 134250496 | bytes 1639559 | solution.py:45
  71.7 2.0 fusion.26
  76.4 2.0 fusion.26
  85.8 2.0 fusion.26
  90.5 2.0 fusion.26
  99.9 2.0 fusion.26
  104.7 2.0 fusion.26
  114.1 2.0 fusion.26
  118.8 2.0 fusion.26
  128.2 2.0 fusion.26
  134.9 5.7 %convolution_convert_fusion.1 = bf16[128,256,128]{2,0,1:T(8,128)(2,1)} fusion(s32[16]{0:T(128)S(1)} %dynamic-slice_bitcast_fusion, bf16[2,8,256,128]{3,2,1,0:T(8,128)(2,1)S(1)} %bitcast.88), kind=kOutput, calls=%fused_computation.8 | convolution fusion | flops 138414080 | bytes 9437248 | tf_op jit(solution)/shard_map/dot_general | solution.py:62
  142.6 152.3 %all-reduce.3.cloned.1.call-done = bf16[128,256,128]{2,0,1:T(8,128)(2,1)} async-done(((bf16[128,256,128]{2,0,1:T(8,128)(2,1)}), bf16[128,256,128]{2,0,1:T(8,128)(2,1)}) %all-reduce.3.cloned.1.call-update) | async-done | bytes 8388624
  296.3 25.3 %psum.7 = f32[3,56]{1,0:T(4,128)} all-reduce(f32[3,56]{1,0:T(4,128)S(1)} %convolution_bitcast_fusion), channel_id=1, replica_groups=mesh['grid'=16,'band'=8,'pole'=2] {'band','pole'}, use_global_device_ids=true, to_apply=%region_3.4 | all-reduce | flops 168 | bytes 1344 | tf_op jit(solution)/shard_map/psum | solution.py:75
  (62 shorter events, 34.1 us)
Async XLA Ops:
  6.5 25.2 %copy-start = (s32[16,16]{1,0:T(8,128)S(1)}, s32[16,16]{1,0:T(8,128)}, u32[]{:S(2)}) copy-start(s32[16,16]{1,0:T(8,128)} %param.12) | copy-start | bytes 3076
  6.5 10.8 %copy-start.2 = (bf16[1,64,4,16,256]{4,3,2,1,0:T(8,128)(2,1)S(1)}, bf16[1,64,4,16,256]{4,3,2,1,0:T(8,128)(2,1)}, u32[]{:S(2)}) copy-start(bf16[1,64,4,16,256]{4,3,2,1,0:T(8,128)(2,1)} %param.9) | copy-start | bytes 6291460
  6.5 288.3 %all-reduce.3.cloned.1.call-start = ((), (), s32[]{:S(2)}) async-start(), calls=%async_computation | async-start | bytes 16777216
  9.0 30.9 %collective-permute-start = (bf16[1,64,1,16,256]{4,3,2,1,0:T(8,128)(2,1)}, bf16[1,64,1,16,256]{4,3,2,1,0:T(8,128)(2,1)}, u32[]{:S(2)}, u32[]{:S(2)}) collective-permute-start(bf16[1,64,1,16,256]{4,3,2,1,0:T(8,128)(2,1)} %get-tuple-element.43), channel_id=1, source_target_pairs={{16,0},{32,16},{48,32},{64,48},{80,64},{96,80},{112,96},{128,112},... | collective-permute-start | bytes 1572872 | tf_op jit(solution)/shard_map/ppermute | solution.py:17
  14.7 25.2 %collective-permute-start.1 = (bf16[1,64,1,16,256]{4,3,2,1,0:T(8,128)(2,1)}, bf16[1,64,1,16,256]{4,3,2,1,0:T(8,128)(2,1)}, u32[]{:S(2)}, u32[]{:S(2)}) collective-permute-start(bf16[1,64,1,16,256]{4,3,2,1,0:T(8,128)(2,1)} %get-tuple-element.44), channel_id=1, source_target_pairs={{0,16},{16,32},{32,48},{48,64},{64,80},{80,96},{96,112},{112,128},... | collective-permute-start | bytes 1572872 | tf_op jit(solution)/shard_map/ppermute | solution.py:16
  36.3 1.2 copy-start.3
  45.9 13.6 %copy-start.4 = (bf16[16,256,128]{2,1,0:T(8,128)(2,1)S(1)}, bf16[16,256,128]{2,1,0:T(8,128)(2,1)}, u32[]{:S(2)}) copy-start(bf16[16,256,128]{2,1,0:T(8,128)(2,1)} %custom-call) | copy-start | bytes 3145732
  45.9 13.6 %copy-start.7 = (s32[16]{0:T(128)S(1)}, s32[16]{0:T(128)}, u32[]{:S(2)}) copy-start(s32[16]{0:T(128)} %param.11) | copy-start | bytes 196
  140.6 181.0 %copy-start.1 = (s32[16,16]{1,0:T(8,128)S(1)}, s32[16,16]{1,0:T(8,128)}, u32[]{:S(2)}) copy-start(s32[16,16]{1,0:T(8,128)} %param.12) | copy-start | bytes 3076
  140.6 0.7 copy-start.8
  140.6 2.0 copy-start.5
  140.6 155.5 %copy-start.6 = (s32[8,128]{1,0:T(8,128)S(1)}, s32[8,128]{1,0:T(8,128)}, u32[]{:S(2)}) copy-start(s32[8,128]{1,0:T(8,128)} %param.15) | copy-start | bytes 12292
Sparse Core Ops, SparseCore 0:
  140.7 154.1 all-reduce.2
where the time goes:
time: 330 us; the launch traced here: 328 us
  waiting for transfers between devices  152 us (46%)
  local copies, waits for them, and re-layouts  46.6 us (14%)
  matrix products  37.1 us (11%)
  loops' own time  33.5 us (10%)
  blocking collectives  25.3 us (8%)
  between operations  14.9 us (5%)
  other arithmetic  12.9 us (4%)
  starting transfers between devices  5.75 us (2%)
    unnamed x2, waiting for transfers between devices  152 us
    another operation x1, loops' own time, slot_products(): return lax.map(one_slot, (projector, offsets))  33.5 us
    dot_general x16, matrix products, one_slot(): lax.dot_general(window, block_vals, (((1,), (1,)), ((), ())), preferred_e...  31.3 us
    psum x1, blocking collectives, per_device(): return lax.psum(partial_forces, ('band', 'pole'))  25.3 us
    reshape x1, local copies, waits for them, and re-layouts, build_fields(): return stacked.reshape(4 * middle.shape[0] * middle.shape[1], -1)  13.6 us
    dynamic_slice x16, local copies, waits for them, and re-layouts, slot_products(): return lax.map(one_slot, (projector, offsets))  10.6 us
    convert_element_type x2, other arithmetic, derivative(): ((upper.astype(jnp.float32) - lower.astype(jnp.float32)) * 0.5).astype(jn...  6.84 us
  transfers between devices with their start and end apart: 3, of which 1 were waited for; matrix products, arithmetic and copies ran while one was open for 8% of the time, Pallas kernels for 0%

commit v1 on v0

v1 whole, which is shorter than its diff:
```python
import jax
import jax.numpy as jnp
from jax import lax
from jax.experimental import pallas as pl
from jax.experimental.pallas import tpu as pltpu
from jax.sharding import PartitionSpec as P

ATOM_OWN = 56
LANES = 128
BF = jnp.bfloat16
F32 = jnp.float32


def shifted(p_ref, shift, chunks):
    lane = lax.broadcasted_iota(jnp.int32, (p_ref.shape[1], LANES), 1)
    low = lane < shift
    rolled = [
        pltpu.roll(p_ref[0, :, j * LANES : (j + 1) * LANES], shift, 1) for j in range(chunks)
    ]
    zero = jnp.zeros_like(rolled[0])
    pieces = [jnp.where(low, zero, rolled[0])]
    for j in range(1, chunks):
        pieces.append(jnp.where(low, rolled[j - 1], rolled[j]))
    pieces.append(jnp.where(low, rolled[-1], zero))
    return jnp.concatenate(pieces, axis=1)


def window_of(field_ref, first, chunks):
    last = field_ref.shape[0] - 1
    parts = [field_ref[first + j] for j in range(chunks)]
    parts.append(field_ref[jnp.minimum(first + chunks, last)])
    return jnp.concatenate(parts, axis=1)


def contract(a, b):
    return lax.dot_general(a, b, (((1,), (1,)), ((), ())), preferred_element_type=F32)


def value_kernel(off_ref, x_ref, p_ref, xr_ref, lo_ref, hi_ref, c_ref, stage, c32):
    k = pl.program_id(0)
    slots = pl.num_programs(0)
    cols, planes, ny, nz = x_ref.shape
    halves = nz // LANES
    chunks = p_ref.shape[2] // LANES
    per_plane = ny * halves

    @pl.when(k == 0)
    def _():
        for x in range(planes):
            for half in range(halves):
                piece = x_ref[:, x, :, half * LANES : (half + 1) * LANES].astype(F32)
                stage[half] = piece.reshape(cols * ny, LANES)
                for y in range(ny):
                    row = stage[half, pl.ds(y, cols, stride=ny), :].astype(BF)
                    h = (x * ny + y) * halves + half
                    xr_ref[h] = row
                    if x == 0:
                        lo_ref[h] = row
                    if x == planes - 1:
                        hi_ref[h - x * per_plane] = row

    off = off_ref[k]
    proj = shifted(p_ref, off & (LANES - 1), chunks)
    field = window_of(xr_ref, off >> 7, chunks)
    c32[pl.ds(pl.multiple_of(k * cols, cols), cols), :] = contract(field, proj)

    @pl.when(k == slots - 1)
    def _():
        dests = c_ref.shape[0]
        per = cols // dests
        for j in range(cols):
            row = c32[pl.ds(j, dests, stride=cols), :]
            c_ref[j // per, :, (j % per) * LANES : (j % per + 1) * LANES] = row.astype(BF)


def force_kernel(
    off_ref, blk_ref, brick_ref, w_ref, xr_ref, before_ref, after_ref, p_ref, c_ref, t_ref, fields, e32
):
    k = pl.program_id(0)
    slots = pl.num_programs(0)
    rows, cols, _ = xr_ref.shape
    per_plane = before_ref.shape[0]
    chunks = p_ref.shape[2] // LANES

    @pl.when(k == 0)
    def _():
        lane = lax.broadcasted_iota(jnp.int32, (cols, LANES), 1)

        def pair(r, carry):
            y_pair = r % (per_plane // 2)
            base = r - y_pair
            up = 2 * (base + (y_pair + 1) % (per_plane // 2))
            down = 2 * (base + (y_pair + per_plane // 2 - 1) % (per_plane // 2))
            h = 2 * r
            for half in range(2):
                fields[h + half, cols : 2 * cols] = xr_ref[up + half] - xr_ref[down + half]
            a = xr_ref[h]
            b = xr_ref[h + 1]
            a_up = pltpu.roll(a, LANES - 1, 1)
            b_up = pltpu.roll(b, LANES - 1, 1)
            a_down = pltpu.roll(a, 1, 1)
            b_down = pltpu.roll(b, 1, 1)
            last = lane == LANES - 1
            first = lane == 0
            fields[h, 2 * cols :] = jnp.where(last, b_up, a_up) - jnp.where(first, b_down, a_down)
            fields[h + 1, 2 * cols :] = jnp.where(last, a_up, b_up) - jnp.where(first, a_down, b_down)
            return carry

        lax.fori_loop(0, rows // 2, pair, 0)

        def inner(h, carry):
            fields[h, :cols] = xr_ref[h + per_plane] - xr_ref[h - per_plane]
            return carry

        lax.fori_loop(per_plane, rows - per_plane, inner, 0)

        def edge(h, carry):
            fields[h, :cols] = xr_ref[h + per_plane] - before_ref[h]
            t = rows - per_plane + h
            fields[t, :cols] = after_ref[h] - xr_ref[t - per_plane]
            return carry

        lax.fori_loop(0, per_plane, edge, 0)

    off = off_ref[k]
    proj = shifted(p_ref, off & (LANES - 1), chunks)
    field = window_of(fields, off >> 7, chunks)
    e32[pl.ds(pl.multiple_of(k * 3 * cols, 3 * cols), 3 * cols), :] = contract(field, proj)

    @pl.when(k == slots - 1)
    def _():
        n_slots = blk_ref.shape[1]
        per = cols // c_ref.shape[0]
        w = w_ref[0]
        sums = [jnp.zeros((n_slots, LANES), F32) for _ in range(3)]
        for j in range(cols):
            c = c_ref[j // per, :, (j % per) * LANES : (j % per + 1) * LANES].astype(F32)
            for x in range(3):
                sums[x] = sums[x] + c * e32[pl.ds(x * cols + j, n_slots, stride=3 * cols), :]
        t_ref[...] = jnp.zeros(t_ref.shape, F32)
        owned = t_ref.shape[1]
        brick = brick_ref[0]
        place = lax.broadcasted_iota(jnp.int32, (owned, 3 * LANES), 0)
        both = jnp.concatenate(sums, axis=1) * w
        for s in range(n_slots):
            g = blk_ref[brick, s]
            o = g // owned
            t_ref[o] = t_ref[o] + jnp.where(place == g % owned, both[s : s + 1], 0.0)


def owner_kernel(t_ref, coef_ref, atom_ref, out_ref):
    owned = coef_ref.shape[0]
    scale = -coef_ref[...]
    atom_id = lax.broadcasted_iota(jnp.int32, (LANES, LANES), 0)
    total = t_ref[0]
    for s in range(1, t_ref.shape[0]):
        total = total + t_ref[s]
    hits = [atom_ref[b : b + 1, :] == atom_id for b in range(owned)]
    row = lax.broadcasted_iota(jnp.int32, (8, LANES), 0)
    ones = jnp.ones((8, LANES), F32)
    out = jnp.zeros((8, LANES), F32)
    for x in range(3):
        terms = total[:, x * LANES : (x + 1) * LANES] * scale
        acc = jnp.zeros((LANES, LANES), F32)
        for b in range(owned):
            acc = acc + jnp.where(hits[b], terms[b : b + 1, :], 0.0)
        sums = lax.dot_general(
            ones, acc, (((1,), (1,)), ((), ())),
            preferred_element_type=F32, precision=lax.Precision.HIGHEST,
        )
        out = jnp.where(row == x, sums, out)
    for d in range(out_ref.shape[0]):
        out_ref[d] = out


def whole(shape):
    zeros = (0,) * len(shape)
    return pl.BlockSpec(shape, lambda k, *_: zeros)


def per_device(solution, proj_vals, slot_offset, slot_block, proj_coef, pole_weight, proj_atom):
    _, cols, planes, ny, nz = solution.shape
    slots, proj, win = proj_vals.shape
    bricks = lax.axis_size("grid")
    owned = proj_coef.shape[0]
    rows = planes * ny * nz // LANES
    per_plane = rows // planes
    per = cols // bricks
    brick = lax.axis_index("grid").astype(jnp.int32)
    x = solution.reshape(cols, planes, ny, nz)
    p_spec = pl.BlockSpec((1, proj, win), lambda k, *_: (k, 0, 0))

    xr, lo, hi, c_part = pl.pallas_call(
        value_kernel,
        out_shape=(
            jax.ShapeDtypeStruct((rows, cols, LANES), BF),
            jax.ShapeDtypeStruct((per_plane, cols, LANES), BF),
            jax.ShapeDtypeStruct((per_plane, cols, LANES), BF),
            jax.ShapeDtypeStruct((bricks, slots, per * LANES), BF),
        ),
        grid_spec=pltpu.PrefetchScalarGridSpec(
            num_scalar_prefetch=1,
            grid=(slots,),
            in_specs=[whole(x.shape), p_spec],
            out_specs=[
                whole((rows, cols, LANES)),
                whole((per_plane, cols, LANES)),
                whole((per_plane, cols, LANES)),
                whole((bricks, slots, per * LANES)),
            ],
            scratch_shapes=[
                pltpu.VMEM((nz // LANES, cols * ny, LANES), F32),
                pltpu.VMEM((slots * cols, LANES), F32),
            ],
        ),
        compiler_params=pltpu.CompilerParams(vmem_limit_bytes=48 << 20),
        name="values",
    )(slot_offset, x, proj_vals)

    up = [(i, (i + 1) % bricks) for i in range(bricks)]
    down = [(j, i) for i, j in up]
    before = lax.ppermute(hi, "grid", up)
    after = lax.ppermute(lo, "grid", down)

    arrived = lax.all_to_all(c_part, "grid", 0, 0, tiled=True)
    ids = slot_block.reshape(-1)
    same = (ids[:, None] == ids[None, :]).astype(BF)
    summed = jnp.dot(
        same, arrived.reshape(bricks * slots, per * LANES), preferred_element_type=F32
    ).astype(BF)
    coefs = lax.all_to_all(
        summed.reshape(bricks, slots, per * LANES), "grid", 0, 0, tiled=True
    )

    terms = pl.pallas_call(
        force_kernel,
        out_shape=jax.ShapeDtypeStruct((bricks, owned, 3 * LANES), F32),
        grid_spec=pltpu.PrefetchScalarGridSpec(
            num_scalar_prefetch=4,
            grid=(slots,),
            in_specs=[
                whole((rows, cols, LANES)),
                whole((per_plane, cols, LANES)),
                whole((per_plane, cols, LANES)),
                p_spec,
                whole((bricks, slots, per * LANES)),
            ],
            out_specs=whole((bricks, owned, 3 * LANES)),
            scratch_shapes=[
                pltpu.VMEM((rows, 3 * cols, LANES), BF),
                pltpu.VMEM((slots * 3 * cols, LANES), F32),
            ],
        ),
        compiler_params=pltpu.CompilerParams(vmem_limit_bytes=48 << 20),
        name="derivatives",
    )(slot_offset, slot_block, brick[None], pole_weight, xr, before, after, proj_vals, coefs)

    at_owner = lax.all_to_all(terms, "grid", 0, 0, tiled=True)
    copies = lax.axis_size("band") * lax.axis_size("pole")
    shares = pl.pallas_call(
        owner_kernel,
        out_shape=jax.ShapeDtypeStruct((copies, 8, LANES), F32),
        name="owner",
    )(at_owner, proj_coef, proj_atom)
    gathered = lax.all_to_all(shares, ("band", "pole"), 0, 0, tiled=True)
    return jnp.sum(gathered[:, :3, :ATOM_OWN], axis=0)


def solution(mesh):
    placed = (
        P("pole", "band", "grid", None, None),
        P("grid", None, None),
        P("grid"),
        P(),
        P("grid", None),
        P("pole"),
        P("grid", None),
    )
    return jax.shard_map(
        per_device, mesh=mesh, in_specs=placed, out_specs=P(None, "grid"), check_vma=False
    )
```

time: 330 us -> 103 us (0.31)
  waiting for transfers between devices: 152 us -> 10.7 us
  local copies, waits for them, and re-layouts: 46.6 us -> 2.34 us
  Pallas kernels: 0 us -> 38.8 us
  matrix products: 37.1 us -> 1.94 us
  loops' own time: 33.5 us -> 0 us
  between operations: 14.9 us -> 0.7 us
  other arithmetic: 12.9 us -> 0.6 us
  starting transfers between devices: 5.75 us -> 16 us
  blocking collectives: 25.3 us -> 31.3 us
    unnamed x2 -> x0, waiting for transfers between devices: 152 us -> none
    pallas_call x0 -> x3, Pallas kernels: none -> 38.8 us  [the longest x1 21.1 us: per_device(): pl.pallas_call(force_kernel, out_shape=jax.ShapeDtypeStruct((bricks, owne...]
    dot_general x18 -> x1, matrix products: 37.1 us -> 1.94 us  [per_device(): jnp.dot(same, arrived.reshape(bricks * slots, per * LANES), preferred_ele...]
    another operation x1 -> x0, loops' own time: 33.5 us -> none  [slot_products(): return lax.map(one_slot, (projector, offsets))]
    all_to_all x0 -> x2, blocking collectives: none -> 31.3 us  [the longest x1 20.9 us: per_device(): gathered = lax.all_to_all(shares, ('band', 'pole'), 0, 0, tiled=True)]
    psum x1 -> x0, blocking collectives: 25.3 us -> none  [per_device(): return lax.psum(partial_forces, ('band', 'pole'))]
    reshape x1 -> x0, local copies, waits for them, and re-layouts: 13.6 us -> none  [build_fields(): return stacked.reshape(4 * middle.shape[0] * middle.shape[1], -1)]
    all_to_all x0 -> x2, starting transfers between devices: none -> 11.2 us  [the longest x1 7.63 us: per_device(): arrived = lax.all_to_all(c_part, 'grid', 0, 0, tiled=True)]
  transfers between devices with their start and end apart: 3 -> 4, of which waited for: 1 -> 2; matrix products, arithmetic and copies ran while one was open for 8% -> 2% of each run, Pallas kernels for 0% -> 0%
where the time goes in v1:
time: 103 us; the launch traced here: 102 us
  Pallas kernels  38.8 us (38%)
  blocking collectives  31.3 us (30%)
  starting transfers between devices  16 us (16%)
  waiting for transfers between devices  10.7 us (10%)
  local copies, waits for them, and re-layouts  2.34 us (2%)
  matrix products  1.94 us (2%)
    pallas_call x1, Pallas kernels, per_device(): pl.pallas_call(force_kernel, out_shape=jax.ShapeDtypeStruct((bricks, owne...  21.1 us
    all_to_all x1, blocking collectives, per_device(): gathered = lax.all_to_all(shares, ('band', 'pole'), 0, 0, tiled=True)  20.9 us
    pallas_call x1, Pallas kernels, per_device(): pl.pallas_call(value_kernel, out_shape=(jax.ShapeDtypeStruct((rows, cols,...  15.6 us
    all_to_all x1, blocking collectives, per_device(): at_owner = lax.all_to_all(terms, 'grid', 0, 0, tiled=True)  10.5 us
    all_to_all x1, waiting for transfers between devices, per_device(): lax.all_to_all(summed.reshape(bricks, slots, per * LANES), 'grid', 0, 0,...  7.92 us
    all_to_all x1, starting transfers between devices, per_device(): arrived = lax.all_to_all(c_part, 'grid', 0, 0, tiled=True)  7.63 us
    all_to_all x1, starting transfers between devices, per_device(): lax.all_to_all(summed.reshape(bricks, slots, per * LANES), 'grid', 0, 0,...  3.53 us
    ppermute x1, starting transfers between devices, per_device(): after = lax.ppermute(lo, 'grid', down)  3.48 us
  transfers between devices with their start and end apart: 4, of which 2 were waited for; matrix products, arithmetic and copies ran while one was open for 2% of the time, Pallas kernels for 0%

profile of v1, /device:TPU:1, one launch (start us, length us, event | category | flops | bytes accessed | tf_op | source)
XLA Modules:
  0.0 102.4 jit_solution(16018805808123208415)
XLA Ops:
  0.0 0.0 copy-start
  0.0 1.6 %copy-done = bf16[1,64,4,16,256]{4,3,2,1,0:T(8,128)(2,1)S(1)} copy-done((bf16[1,64,4,16,256]{4,3,2,1,0:T(8,128)(2,1)S(1)}, bf16[1,64,4,16,256]{4,3,2,1,0:T(8,128)(2,1)}, u32[]{:S(2)}) %copy-start) | copy-done | bytes 2097176
  1.6 0.0 copy-start.2
  1.6 0.7 copy-done.2
  2.2 0.0 copy-start.1
  2.3 15.6 %values.1 = (bf16[128,64,128]{2,1,0:T(8,128)(2,1)S(1)}, bf16[32,64,128]{2,1,0:T(8,128)(2,1)S(1)}, bf16[32,64,128]{2,1,0:T(8,128)(2,1)}, bf16[16,16,512]{2,1,0:T(8,128)(2,1)}) custom-call(s32[16]{0:T(128)S(1)} %copy-done.2, bf16[64,4,16,256]{3,2,1,0:T(8,128)(2,1)S(1)} %bitcast.5, bf16[16,128,2048]{2,1,0:T(8,128)(2,1)} %p_ref.3), custom_call_target="tpu_custom_call" | custom-call | tf_op jit(solution)/shard_map/values/pallas_call | solution.py:193
  17.9 7.6 %all-to-all-start = ((bf16[16,16,512]{2,1,0:T(8,128)(2,1)}), bf16[16,16,512]{2,1,0:T(8,128)(2,1)}, u32[]{:S(2)}, u32[]{:S(2)}) async-start(bf16[16,16,512]{2,1,0:T(8,128)(2,1)} %get-tuple-element.12), calls=%async_computation | async-start | bytes 524288 | tf_op jit(solution)/shard_map/all_to_all | solution.py:225
  25.5 0.0 copy-done.4
  25.5 1.4 %collective-permute-start = (bf16[32,64,128]{2,1,0:T(8,128)(2,1)}, bf16[32,64,128]{2,1,0:T(8,128)(2,1)S(1)}, u32[]{:S(2)}, u32[]{:S(2)}) collective-permute-start(bf16[32,64,128]{2,1,0:T(8,128)(2,1)} %get-tuple-element.10), channel_id=1, source_target_pairs={{0,16},{16,32},{32,48},{48,64},{64,80},{80,96},{96,112},{112,128},... | collective-permute-start | bytes 1572872 | tf_op jit(solution)/shard_map/ppermute | solution.py:222
  26.9 3.5 %collective-permute-start.1 = (bf16[32,64,128]{2,1,0:T(8,128)(2,1)}, bf16[32,64,128]{2,1,0:T(8,128)(2,1)S(1)}, u32[]{:S(2)}, u32[]{:S(2)}) collective-permute-start(bf16[32,64,128]{2,1,0:T(8,128)(2,1)} %copy-done.4), channel_id=1, source_target_pairs={{16,0},{32,16},{48,32},{64,48},{80,64},{96,80},{112,96},{128,112},... | collective-permute-start | bytes 1572872 | tf_op jit(solution)/shard_map/ppermute | solution.py:223
  30.4 0.0 copy-done.1
  30.4 0.1 eq.15
  30.4 2.8 %all-to-all-done = bf16[16,16,512]{2,1,0:T(8,128)(2,1)} async-done(((bf16[16,16,512]{2,1,0:T(8,128)(2,1)}), bf16[16,16,512]{2,1,0:T(8,128)(2,1)}, u32[]{:S(2)}, u32[]{:S(2)}) %all-to-all-start) | async-done | bytes 262176 | tf_op jit(solution)/shard_map/all_to_all | solution.py:225
  33.2 1.9 %convolution_convert_fusion = bf16[256,512]{1,0:T(8,128)(2,1)} fusion(bf16[256,512]{1,0:T(8,128)(2,1)} %bitcast.2, s32[256]{0:T(256)S(1)} %eq.15), kind=kOutput, calls=%fused_computation | convolution fusion | flops 67305472 | bytes 525312 | tf_op jit(solution)/shard_map/dot_general | solution.py:228
  35.1 3.5 %all-to-all-start.1 = ((bf16[16,16,512]{2,1,0:T(8,128)(2,1)}), bf16[16,16,512]{2,1,0:T(8,128)(2,1)S(1)}, u32[]{:S(2)}, u32[]{:S(2)}) async-start(bf16[16,16,512]{2,1,0:T(8,128)(2,1)} %bitcast.6), calls=%async_computation.1 | async-start | bytes 524288 | tf_op jit(solution)/shard_map/all_to_all | solution.py:231
  39.3 7.9 %all-to-all-done.1.c_ref = bf16[16,16,512]{2,1,0:T(8,128)(2,1)S(1)} async-done(((bf16[16,16,512]{2,1,0:T(8,128)(2,1)}), bf16[16,16,512]{2,1,0:T(8,128)(2,1)S(1)}, u32[]{:S(2)}, u32[]{:S(2)}) %all-to-all-start.1) | async-done | bytes 262176 | tf_op jit(solution)/shard_map/all_to_all | solution.py:231
  47.3 0.0 collective-permute-done.before_ref
  47.3 0.0 collective-permute-done.1.after_ref
  47.3 0.0 copy-done.3
  47.3 21.1 %derivatives.1 = f32[16,8,384]{2,1,0:T(8,128)S(1)} custom-call(s32[16]{0:T(128)S(1)} %copy-done.3, s32[16,16]{1,0:T(8,128)S(1)} %copy-done.1, s32[1]{0:T(128)} %bitcast.brick_ref, f32[1]{0:T(128)S(6)} %copy.8.w_ref, bf16[128,64,128]{2,1,0:T(8,128)(2,1)S(1)} %get-tuple-element.9.xr_ref, bf16[32,64,128]{2,1,0:T(8,128)(2,1)S(1)} %collective-permute-done.before_ref, ...), custom_call_target="tpu_custom_call" | custom-call | tf_op jit(solution)/shard_map/derivatives/pallas_call | solution.py:235
  68.4 10.5 %all_to_all.20.t_ref = f32[16,8,384]{2,1,0:T(8,128)} all-to-all(f32[16,8,384]{2,1,0:T(8,128)S(1)} %derivatives.1), channel_id=1, replica_groups=mesh['grid'=16,'band'=8,'pole'=2] {'grid'}, dimensions={0} | all-to-all | bytes 393216 | tf_op jit(solution)/shard_map/all_to_all | solution.py:258
  78.9 2.1 %owner.1 = f32[16,8,128]{2,1,0:T(8,128)} custom-call(f32[16,8,384]{2,1,0:T(8,128)} %all_to_all.20.t_ref, f32[8,128]{1,0:T(8,128)} %coef_ref.1, s32[8,128]{1,0:T(8,128)} %atom_ref.1), custom_call_target="tpu_custom_call" | custom-call | tf_op jit(solution)/shard_map/owner/pallas_call | solution.py:260
  81.0 20.9 %all_to_all.21 = f32[16,8,128]{2,1,0:T(8,128)S(1)} all-to-all(f32[16,8,128]{2,1,0:T(8,128)} %owner.1), channel_id=1, replica_groups=mesh['grid'=16,'band'=8,'pole'=2] {'band','pole'}, dimensions={0} | all-to-all | bytes 131072 | tf_op jit(solution)/shard_map/all_to_all | solution.py:265
  101.8 0.6 slice_reduce_fusion
  (2 shorter events, 0.0 us)
Async XLA Ops:
  0.0 1.6 %copy-start = (bf16[1,64,4,16,256]{4,3,2,1,0:T(8,128)(2,1)S(1)}, bf16[1,64,4,16,256]{4,3,2,1,0:T(8,128)(2,1)}, u32[]{:S(2)}) copy-start(bf16[1,64,4,16,256]{4,3,2,1,0:T(8,128)(2,1)} %param.7) | copy-start | bytes 6291460
  1.6 0.7 copy-start.2
  2.2 28.1 %copy-start.1 = (s32[16,16]{1,0:T(8,128)S(1)}, s32[16,16]{1,0:T(8,128)}, u32[]{:S(2)}) copy-start(s32[16,16]{1,0:T(8,128)} %blk_ref.1) | copy-start | bytes 3076
  2.2 45.0 %copy-start.3 = (s32[16]{0:T(128)S(1)}, s32[16]{0:T(128)}, u32[]{:S(2)}) copy-start(s32[16]{0:T(128)} %off_ref.3) | copy-start | bytes 196
  17.9 7.6 %copy-start.4 = (bf16[32,64,128]{2,1,0:T(8,128)(2,1)}, bf16[32,64,128]{2,1,0:T(8,128)(2,1)S(1)}, u32[]{:S(2)}) copy-start(bf16[32,64,128]{2,1,0:T(8,128)(2,1)S(1)} %get-tuple-element.11) | copy-start | bytes 1572868
  17.9 15.3 %all-to-all-start = ((bf16[16,16,512]{2,1,0:T(8,128)(2,1)}), bf16[16,16,512]{2,1,0:T(8,128)(2,1)}, u32[]{:S(2)}, u32[]{:S(2)}) async-start(bf16[16,16,512]{2,1,0:T(8,128)(2,1)} %get-tuple-element.12), calls=%async_computation | async-start | bytes 524288 | tf_op jit(solution)/shard_map/all_to_all | solution.py:225
  25.5 21.8 %collective-permute-start = (bf16[32,64,128]{2,1,0:T(8,128)(2,1)}, bf16[32,64,128]{2,1,0:T(8,128)(2,1)S(1)}, u32[]{:S(2)}, u32[]{:S(2)}) collective-permute-start(bf16[32,64,128]{2,1,0:T(8,128)(2,1)} %get-tuple-element.10), channel_id=1, source_target_pairs={{0,16},{16,32},{32,48},{48,64},{64,80},{80,96},{96,112},{112,128},... | collective-permute-start | bytes 1572872 | tf_op jit(solution)/shard_map/ppermute | solution.py:222
  26.9 20.4 %collective-permute-start.1 = (bf16[32,64,128]{2,1,0:T(8,128)(2,1)}, bf16[32,64,128]{2,1,0:T(8,128)(2,1)S(1)}, u32[]{:S(2)}, u32[]{:S(2)}) collective-permute-start(bf16[32,64,128]{2,1,0:T(8,128)(2,1)} %copy-done.4), channel_id=1, source_target_pairs={{16,0},{32,16},{48,32},{64,48},{80,64},{96,80},{112,96},{128,112},... | collective-permute-start | bytes 1572872 | tf_op jit(solution)/shard_map/ppermute | solution.py:223
  35.1 12.1 %all-to-all-start.1 = ((bf16[16,16,512]{2,1,0:T(8,128)(2,1)}), bf16[16,16,512]{2,1,0:T(8,128)(2,1)S(1)}, u32[]{:S(2)}, u32[]{:S(2)}) async-start(bf16[16,16,512]{2,1,0:T(8,128)(2,1)} %bitcast.6), calls=%async_computation.1 | async-start | bytes 524288 | tf_op jit(solution)/shard_map/all_to_all | solution.py:231

commit v2 on v1

v2 whole, which is shorter than its diff:
```python
import jax
import jax.numpy as jnp
from jax import lax
from jax.experimental import pallas as pl
from jax.experimental.pallas import tpu as pltpu
from jax.sharding import PartitionSpec as P

ATOM_OWN = 56
LANES = 128
BF = jnp.bfloat16
LIMIT = 57
NY = 16
GROUP = 8
VALUE_GROUP = 4
AHEAD = 8
GROUP_COLS = 16
F32 = jnp.float32


def shifted(block, shift, chunks):
    lane = lax.broadcasted_iota(jnp.int32, (block.shape[0], LANES), 1)
    low = lane < shift
    rolled = [
        pltpu.roll(block[:, j * LANES : (j + 1) * LANES], shift, 1) for j in range(chunks)
    ]
    zero = jnp.zeros_like(rolled[0])
    pieces = [jnp.where(low, zero, rolled[0])]
    for j in range(1, chunks):
        pieces.append(jnp.where(low, rolled[j - 1], rolled[j]))
    pieces.append(jnp.where(low, rolled[-1], zero))
    return jnp.concatenate(pieces, axis=1)


def window_of(field_ref, first, chunks):
    last = field_ref.shape[0] - 1
    parts = [field_ref[first + j] for j in range(chunks - 1)]
    parts.append(field_ref[jnp.minimum(first + chunks - 1, last)])
    return jnp.concatenate(parts, axis=1)


def contract(a, b):
    return lax.dot_general(a, b, (((1,), (1,)), ((), ())), preferred_element_type=F32)


def value_kernel(
    off_hbm, x_hbm, p_hbm, xr_hbm, lo_hbm, hi_hbm, c_ref, off, xbuf, pbuf, xr, stage, c32, osem, xsem, psem, rsem
):
    cols, planes, ny, nz = xbuf.shape
    slots = pbuf.shape[0]
    halves = nz // LANES
    chunks = pbuf.shape[2] // LANES
    per_plane = ny * halves

    def x_copy(g):
        part = pl.ds(g * GROUP_COLS, GROUP_COLS)
        return pltpu.make_async_copy(x_hbm.at[part], xbuf.at[part], xsem.at[g])

    def p_copy(k):
        return pltpu.make_async_copy(p_hbm.at[k], pbuf.at[k], psem.at[k])

    def plane(x):
        return pl.ds(x * per_plane, per_plane)

    for g in range(cols // GROUP_COLS):
        x_copy(g).start()
    off_copy = pltpu.make_async_copy(off_hbm, off, osem)
    off_copy.start()
    for k in range(AHEAD):
        p_copy(k).start()
    outgoing = [
        pltpu.make_async_copy(xr, xr_hbm, rsem.at[0]),
        pltpu.make_async_copy(xr.at[plane(0)], lo_hbm, rsem.at[1]),
        pltpu.make_async_copy(xr.at[plane(planes - 1)], hi_hbm, rsem.at[2]),
    ]
    for g in range(cols // GROUP_COLS):
        x_copy(g).wait()
        part = slice(g * GROUP_COLS, (g + 1) * GROUP_COLS)
        for x in range(planes):
            for half in range(halves):
                piece = xbuf[part, x, :, half * LANES : (half + 1) * LANES].astype(F32)
                stage[x, half] = piece.reshape(GROUP_COLS * ny, LANES)
                for y in range(ny):
                    row = stage[x, half, pl.ds(y, GROUP_COLS, stride=ny), :].astype(BF)
                    xr[(x * ny + y) * halves + half, part] = row
    for copy in outgoing:
        copy.start()
    off_copy.wait()

    def group(i, carry):
        for u in range(VALUE_GROUP):
            p_copy(i * VALUE_GROUP + u).wait()

        @pl.when(i * VALUE_GROUP + AHEAD < slots)
        def _():
            for u in range(VALUE_GROUP):
                p_copy(i * VALUE_GROUP + u + AHEAD).start()

        for u in range(VALUE_GROUP):
            k = i * VALUE_GROUP + u
            proj = shifted(pbuf[k], off[k] & (LANES - 1), chunks)
            field = window_of(xr, off[k] >> 7, chunks + 1)
            c32[pl.ds(pl.multiple_of(k * cols, cols), cols), :] = contract(field, proj)
        return carry

    lax.fori_loop(0, slots // VALUE_GROUP, group, 0)

    dests = c_ref.shape[0]
    per = cols // dests
    for j in range(cols):
        row = c32[pl.ds(j, dests, stride=cols), :]
        c_ref[j // per, :, (j % per) * LANES : (j % per + 1) * LANES] = row.astype(BF)
    for copy in outgoing:
        copy.wait()


def fetch_blocks(off_hbm, off, p_hbm, pbuf, osem, psem):
    copies = [
        pltpu.make_async_copy(p_hbm.at[k], pbuf.at[k], psem.at[k]) for k in range(AHEAD)
    ]
    offsets = pltpu.make_async_copy(off_hbm, off, osem)
    offsets.start()
    for copy in copies:
        copy.start()
    return offsets


def partials(off, p_hbm, pbuf, psem, fields, e_ref):
    slots, _, win = pbuf.shape
    chunks = win // LANES

    def p_copy(k):
        return pltpu.make_async_copy(p_hbm.at[k], pbuf.at[k], psem.at[k])

    def group(i, carry):
        for u in range(GROUP):
            p_copy(i * GROUP + u).wait()

        @pl.when(i * GROUP + AHEAD < slots)
        def _():
            for u in range(GROUP):
                p_copy(i * GROUP + u + AHEAD).start()

        for u in range(GROUP):
            k = i * GROUP + u
            proj = shifted(pbuf[k], off[k] & (LANES - 1), chunks)
            field = window_of(fields, off[k] >> 7, chunks + 1)
            e_ref[k] = contract(field, proj).astype(BF)
        return carry

    lax.fori_loop(0, slots // GROUP, group, 0)


def inside_kernel(off_hbm, xr_hbm, p_hbm, e_ref, off, xr, fields, pbuf, osem, xsem, psem):
    rows, cols, _ = xr.shape
    xr_copy = pltpu.make_async_copy(xr_hbm, xr, xsem)
    xr_copy.start()
    offsets = fetch_blocks(off_hbm, off, p_hbm, pbuf, osem, psem)
    lane = lax.broadcasted_iota(jnp.int32, (cols, LANES), 1)
    last = lane == LANES - 1
    first = lane == 0

    def pair(r, carry):
        y = r % NY
        up = 2 * (r - y + (y + 1) % NY)
        down = 2 * (r - y + (y + NY - 1) % NY)
        h = 2 * r
        for half in range(2):
            fields[h + half, :cols] = xr[up + half] - xr[down + half]
        a = xr[h]
        b = xr[h + 1]
        a_up = pltpu.roll(a, LANES - 1, 1)
        b_up = pltpu.roll(b, LANES - 1, 1)
        a_down = pltpu.roll(a, 1, 1)
        b_down = pltpu.roll(b, 1, 1)
        fields[h, cols:] = jnp.where(last, b_up, a_up) - jnp.where(first, b_down, a_down)
        fields[h + 1, cols:] = jnp.where(last, a_up, b_up) - jnp.where(first, a_down, b_down)
        return carry

    xr_copy.wait()
    lax.fori_loop(0, rows // 2, pair, 0, unroll=4)
    offsets.wait()
    partials(off, p_hbm, pbuf, psem, fields, e_ref)


def across_kernel(
    off_hbm, xr_hbm, before_ref, after_ref, p_hbm, e_ref, off, xr, fields, pbuf, osem, xsem, psem
):
    rows = xr.shape[0]
    per_plane = before_ref.shape[0]
    xr_copy = pltpu.make_async_copy(xr_hbm, xr, xsem)
    xr_copy.start()
    offsets = fetch_blocks(off_hbm, off, p_hbm, pbuf, osem, psem)

    def inner(h, carry):
        fields[h] = xr[h + per_plane] - xr[h - per_plane]
        return carry

    def edge(h, carry):
        fields[h] = xr[h + per_plane] - before_ref[h]
        t = rows - per_plane + h
        fields[t] = after_ref[h] - xr[t - per_plane]
        return carry

    xr_copy.wait()
    lax.fori_loop(per_plane, rows - per_plane, inner, 0, unroll=8)
    lax.fori_loop(0, per_plane, edge, 0, unroll=8)
    offsets.wait()
    partials(off, p_hbm, pbuf, psem, fields, e_ref)


def term_kernel(blk_ref, brick_ref, w_ref, c_ref, ex_ref, eyz_ref, t_ref, c32):
    dests, slots, _ = c_ref.shape
    cols = ex_ref.shape[1]
    per = cols // dests
    for j in range(cols):
        c = c_ref[j // per, :, (j % per) * LANES : (j % per + 1) * LANES].astype(F32)
        c32[pl.ds(j, slots, stride=cols), :] = c
    t_ref[...] = jnp.zeros(t_ref.shape, F32)
    owned = t_ref.shape[1]
    brick = brick_ref[0]
    w = w_ref[0]
    place = lax.broadcasted_iota(jnp.int32, (owned, LANES), 0)
    for k in range(slots):
        c = c32[k * cols : (k + 1) * cols] * w
        g = blk_ref[brick, k]
        o = g // owned
        here = place == g % owned
        parts = (ex_ref[k], eyz_ref[k, :cols], eyz_ref[k, cols:])
        for x in range(3):
            term = jnp.sum(c * parts[x].astype(F32), axis=0, keepdims=True)
            at = slice(x * LANES, (x + 1) * LANES)
            t_ref[o, :, at] = t_ref[o, :, at] + jnp.where(here, term, 0.0)


def owner_kernel(t_ref, coef_ref, atom_ref, out_ref):
    owned = coef_ref.shape[0]
    scale = -coef_ref[...]
    atom_id = lax.broadcasted_iota(jnp.int32, (LANES, LANES), 0)
    total = t_ref[0]
    for s in range(1, t_ref.shape[0]):
        total = total + t_ref[s]
    hits = [atom_ref[b : b + 1, :] == atom_id for b in range(owned)]
    row = lax.broadcasted_iota(jnp.int32, (8, LANES), 0)
    ones = jnp.ones((8, LANES), F32)
    out = jnp.zeros((8, LANES), F32)
    for x in range(3):
        terms = total[:, x * LANES : (x + 1) * LANES] * scale
        acc = jnp.zeros((LANES, LANES), F32)
        for b in range(owned):
            acc = acc + jnp.where(hits[b], terms[b : b + 1, :], 0.0)
        sums = lax.dot_general(
            ones, acc, (((1,), (1,)), ((), ())),
            preferred_element_type=F32, precision=lax.Precision.HIGHEST,
        )
        out = jnp.where(row == x, sums, out)
    for d in range(out_ref.shape[0]):
        out_ref[d] = out


def forces(solution, proj_vals, slot_offset, slot_block, proj_coef, pole_weight, proj_atom):
    _, cols, planes, ny, nz = solution.shape
    slots, proj, win = proj_vals.shape
    bricks = lax.axis_size("grid")
    owned = proj_coef.shape[0]
    rows = planes * ny * nz // LANES
    per_plane = rows // planes
    per = cols // bricks
    brick = lax.axis_index("grid").astype(jnp.int32)
    x = solution.reshape(cols, planes, ny, nz)

    def params(mib):
        return pltpu.CompilerParams(vmem_limit_bytes=mib << 20)

    smem = pl.BlockSpec(memory_space=pltpu.SMEM)
    vmem = pl.BlockSpec(memory_space=pltpu.VMEM)
    hbm = pl.BlockSpec(memory_space=pltpu.HBM)

    dma = pltpu.SemaphoreType.DMA
    xr, lo, hi, c_part = pl.pallas_call(
        value_kernel,
        out_shape=(
            jax.ShapeDtypeStruct((rows, cols, LANES), BF),
            jax.ShapeDtypeStruct((per_plane, cols, LANES), BF),
            jax.ShapeDtypeStruct((per_plane, cols, LANES), BF),
            jax.ShapeDtypeStruct((bricks, slots, per * LANES), BF),
        ),
        in_specs=[hbm, hbm, hbm],
        out_specs=[hbm, hbm, hbm, vmem],
        scratch_shapes=[
            pltpu.SMEM((slots,), jnp.int32),
            pltpu.VMEM((cols, planes, ny, nz), BF),
            pltpu.VMEM((slots, proj, win), BF),
            pltpu.VMEM((rows, cols, LANES), BF),
            pltpu.VMEM((planes, nz // LANES, GROUP_COLS * ny, LANES), F32),
            pltpu.VMEM((slots * cols, LANES), F32),
            dma,
            dma((cols // GROUP_COLS,)),
            dma((slots,)),
            dma((3,)),
        ],
        compiler_params=params(LIMIT),
        name="values",
    )(slot_offset, x, proj_vals)

    arrived = lax.all_to_all(c_part, "grid", 0, 0, tiled=True)

    up = [(i, (i + 1) % bricks) for i in range(bricks)]
    down = [(j, i) for i, j in up]
    before = lax.ppermute(hi, "grid", up)
    after = lax.ppermute(lo, "grid", down)

    def scratch(fields):
        return [
            pltpu.SMEM((slots,), jnp.int32),
            pltpu.VMEM((rows, cols, LANES), BF),
            pltpu.VMEM((rows, fields * cols, LANES), BF),
            pltpu.VMEM((slots, proj, win), BF),
            dma,
            dma,
            dma((slots,)),
        ]

    e_yz = pl.pallas_call(
        inside_kernel,
        out_shape=jax.ShapeDtypeStruct((slots, 2 * cols, LANES), BF),
        in_specs=[hbm] * 3,
        out_specs=vmem,
        scratch_shapes=scratch(2),
        compiler_params=params(LIMIT),
        name="inside",
    )(slot_offset, xr, proj_vals)

    arrived, e_yz = lax.optimization_barrier((arrived, e_yz))
    ids = slot_block.reshape(-1)
    same = (ids[:, None] == ids[None, :]).astype(BF)
    summed = jnp.dot(
        same, arrived.reshape(bricks * slots, per * LANES), preferred_element_type=F32
    ).astype(BF)
    coefs = lax.all_to_all(
        summed.reshape(bricks, slots, per * LANES), "grid", 0, 0, tiled=True
    )

    e_x = pl.pallas_call(
        across_kernel,
        out_shape=jax.ShapeDtypeStruct((slots, cols, LANES), BF),
        in_specs=[hbm, hbm, vmem, vmem, hbm],
        out_specs=vmem,
        scratch_shapes=scratch(1),
        compiler_params=params(LIMIT),
        name="across",
    )(slot_offset, xr, before, after, proj_vals)

    terms = pl.pallas_call(
        term_kernel,
        out_shape=jax.ShapeDtypeStruct((bricks, owned, 3 * LANES), F32),
        in_specs=[smem, smem, smem, vmem, vmem, vmem],
        out_specs=vmem,
        scratch_shapes=[pltpu.VMEM((slots * cols, LANES), F32)],
        compiler_params=params(8),
        name="terms",
    )(slot_block, brick[None], pole_weight, coefs, e_x, e_yz)

    at_owner = lax.all_to_all(terms, "grid", 0, 0, tiled=True)
    copies = lax.axis_size("band") * lax.axis_size("pole")
    shares = pl.pallas_call(
        owner_kernel,
        out_shape=jax.ShapeDtypeStruct((copies, 8, LANES), F32),
        name="owner",
    )(at_owner, proj_coef, proj_atom)
    gathered = lax.all_to_all(shares, ("band", "pole"), 0, 0, tiled=True)
    return jnp.sum(gathered[:, :3, :ATOM_OWN], axis=0)


def solution(mesh):
    placed = (
        P("pole", "band", "grid", None, None),
        P("grid", None, None),
        P("grid"),
        P(),
        P("grid", None),
        P("pole"),
        P("grid", None),
    )
    return jax.shard_map(
        forces, mesh=mesh, in_specs=placed, out_specs=P(None, "grid"), check_vma=False
    )
```

time: 103 us -> 86.2 us (0.84)
  waiting for transfers between devices: 10.7 us -> 0.01 us
  Pallas kernels: 38.8 us -> 31.2 us
  blocking collectives: 31.3 us -> 33.5 us
    all_to_all x2, waiting for transfers between devices: 10.7 us -> 0.01 us  [the longest x1 0.01 us: forces(): arrived = lax.all_to_all(c_part, 'grid', 0, 0, tiled=True)]
    pallas_call x3 -> x5, Pallas kernels: 38.8 us -> 31.2 us  [the longest x1 9.57 us: forces(): pl.pallas_call(inside_kernel, out_shape=jax.ShapeDtypeStruct((slots, 2 *...]
    all_to_all x2, blocking collectives: 31.3 us -> 33.5 us  [the longest x1 19.7 us: forces(): gathered = lax.all_to_all(shares, ('band', 'pole'), 0, 0, tiled=True)]
  transfers between devices with their start and end apart: 4 -> 4, of which waited for: 2 -> 0; matrix products, arithmetic and copies ran while one was open for 2% -> 1% of each run, Pallas kernels for 0% -> 22%
where the time goes in v2:
time: 86.2 us; the launch traced here: 85.7 us
  blocking collectives  33.5 us (39%)
  Pallas kernels  31.2 us (36%)
  starting transfers between devices  16 us (19%)
  local copies, waits for them, and re-layouts  2.61 us (3%)
  matrix products  0.98 us (1%)
    all_to_all x1, blocking collectives, forces(): gathered = lax.all_to_all(shares, ('band', 'pole'), 0, 0, tiled=True)  19.7 us
    all_to_all x1, blocking collectives, forces(): at_owner = lax.all_to_all(terms, 'grid', 0, 0, tiled=True)  13.8 us
    pallas_call x1, Pallas kernels, forces(): pl.pallas_call(inside_kernel, out_shape=jax.ShapeDtypeStruct((slots, 2 *...  9.57 us
    pallas_call x1, Pallas kernels, forces(): pl.pallas_call(across_kernel, out_shape=jax.ShapeDtypeStruct((slots, cols...  9.22 us
    pallas_call x1, Pallas kernels, forces(): pl.pallas_call(value_kernel, out_shape=(jax.ShapeDtypeStruct((rows, cols,...  9.02 us
    all_to_all x1, starting transfers between devices, forces(): arrived = lax.all_to_all(c_part, 'grid', 0, 0, tiled=True)  7.59 us
    all_to_all x1, starting transfers between devices, forces(): lax.all_to_all(summed.reshape(bricks, slots, per * LANES), 'grid', 0, 0,...  3.53 us
    ppermute x1, starting transfers between devices, forces(): after = lax.ppermute(lo, 'grid', down)  3.5 us
  transfers between devices with their start and end apart: 4, of which 0 were waited for; matrix products, arithmetic and copies ran while one was open for 1% of the time, Pallas kernels for 22%

profile of v2, /device:TPU:1, one launch (start us, length us, event | category | flops | bytes accessed | tf_op | source)
XLA Modules:
  0.0 85.7 jit_solution(6162329417634240679)
XLA Ops:
  0.0 9.0 %values.1 = (bf16[128,64,128]{2,1,0:T(8,128)(2,1)}, bf16[32,64,128]{2,1,0:T(8,128)(2,1)}, bf16[32,64,128]{2,1,0:T(8,128)(2,1)}, bf16[16,16,512]{2,1,0:T(8,128)(2,1)}) custom-call(s32[16]{0:T(128)} %off_hbm.5, bf16[64,4,16,256]{3,2,1,0:T(8,128)(2,1)} %bitcast.5, bf16[16,128,2048]{2,1,0:T(8,128)(2,1)} %p_hbm.5), custom_call_target="tpu_custom_call" | custom-call | tf_op jit(solution)/shard_map/values/pallas_call | solution.py:279
  9.0 7.6 %all-to-all-start = ((bf16[16,16,512]{2,1,0:T(8,128)(2,1)}), bf16[16,16,512]{2,1,0:T(8,128)(2,1)S(1)}, u32[]{:S(2)}, u32[]{:S(2)}) async-start(bf16[16,16,512]{2,1,0:T(8,128)(2,1)} %get-tuple-element.11), calls=%async_computation | async-start | bytes 524288 | tf_op jit(solution)/shard_map/all_to_all | solution.py:305
  16.6 1.4 %collective-permute-start = (bf16[32,64,128]{2,1,0:T(8,128)(2,1)}, bf16[32,64,128]{2,1,0:T(8,128)(2,1)S(1)}, u32[]{:S(2)}, u32[]{:S(2)}) collective-permute-start(bf16[32,64,128]{2,1,0:T(8,128)(2,1)} %get-tuple-element.14), channel_id=1, source_target_pairs={{0,16},{16,32},{32,48},{48,64},{64,80},{80,96},{96,112},{112,128},... | collective-permute-start | bytes 1572872 | tf_op jit(solution)/shard_map/ppermute | solution.py:309
  18.0 3.5 %collective-permute-start.1 = (bf16[32,64,128]{2,1,0:T(8,128)(2,1)}, bf16[32,64,128]{2,1,0:T(8,128)(2,1)S(1)}, u32[]{:S(2)}, u32[]{:S(2)}) collective-permute-start(bf16[32,64,128]{2,1,0:T(8,128)(2,1)} %get-tuple-element.15), channel_id=1, source_target_pairs={{16,0},{32,16},{48,32},{64,48},{80,64},{96,80},{112,96},{128,112},... | collective-permute-start | bytes 1572872 | tf_op jit(solution)/shard_map/ppermute | solution.py:310
  21.5 9.6 %inside.1.eyz_ref = bf16[16,128,128]{2,1,0:T(8,128)(2,1)} custom-call(s32[16]{0:T(128)} %off_hbm.5, bf16[128,64,128]{2,1,0:T(8,128)(2,1)} %get-tuple-element.12.xr_hbm, bf16[16,128,2048]{2,1,0:T(8,128)(2,1)} %p_hbm.5), custom_call_target="tpu_custom_call" | custom-call | tf_op jit(solution)/shard_map/inside/pallas_call | solution.py:323
  31.1 0.0 copy-done.2
  31.1 0.1 eq.15
  31.2 0.0 all-to-all-done
  31.2 1.0 %convolution_convert_fusion = bf16[256,512]{1,0:T(8,128)(2,1)} fusion(bf16[256,512]{1,0:T(8,128)(2,1)S(1)} %bitcast.6, s32[256]{0:T(256)S(1)} %eq.15), kind=kOutput, calls=%fused_computation | convolution fusion | flops 67305472 | bytes 525312 | tf_op jit(solution)/shard_map/dot_general | solution.py:336
  32.1 3.5 %all-to-all-start.1 = ((bf16[16,16,512]{2,1,0:T(8,128)(2,1)}), bf16[16,16,512]{2,1,0:T(8,128)(2,1)S(1)}, u32[]{:S(2)}, u32[]{:S(2)}) async-start(bf16[16,16,512]{2,1,0:T(8,128)(2,1)} %bitcast.3), calls=%async_computation.1 | async-start | bytes 524288 | tf_op jit(solution)/shard_map/all_to_all | solution.py:339
  36.3 0.0 copy-start
  36.3 0.0 collective-permute-done.before_ref
  36.4 0.0 copy-start.3
  36.4 0.0 collective-permute-done.1.after_ref
  36.4 0.8 copy-done.3
  37.1 0.8 copy-done.4
  37.9 9.2 %across.1.ex_ref = bf16[16,64,128]{2,1,0:T(8,128)(2,1)} custom-call(s32[16]{0:T(128)} %off_hbm.5, bf16[128,64,128]{2,1,0:T(8,128)(2,1)} %get-tuple-element.12.xr_hbm, bf16[32,64,128]{2,1,0:T(8,128)(2,1)} %copy-done.3, bf16[32,64,128]{2,1,0:T(8,128)(2,1)} %copy-done.4, bf16[16,128,2048]{2,1,0:T(8,128)(2,1)} %p_hbm.5), custom_call_target="tpu_custom_call" | custom-call | tf_op jit(solution)/shard_map/across/pallas_call | solution.py:343
  47.2 0.0 all-to-all-done.1.c_ref
  47.2 0.9 %copy-done.1 = bf16[16,64,128]{2,1,0:T(8,128)(2,1)S(1)} copy-done((bf16[16,64,128]{2,1,0:T(8,128)(2,1)S(1)}, bf16[16,64,128]{2,1,0:T(8,128)(2,1)}, u32[]{:S(2)}) %copy-start.1) | copy-done | bytes 262168
  48.1 1.3 %terms.1 = f32[16,8,384]{2,1,0:T(8,128)S(1)} custom-call(s32[16,16]{1,0:T(8,128)S(1)} %copy-done.2, s32[1]{0:T(128)} %bitcast.brick_ref, f32[1]{0:T(128)S(6)} %copy.8.w_ref, bf16[16,16,512]{2,1,0:T(8,128)(2,1)S(1)} %all-to-all-done.1.c_ref, bf16[16,64,128]{2,1,0:T(8,128)(2,1)S(1)} %copy-done.1, bf16[16,128,128]{2,1,0:T(8,128)(2,1)S(1)} %copy-done), custom_call_target="tpu_custom_call" | custom-call | tf_op jit(solution)/shard_map/terms/pallas_call | solution.py:353
  49.5 13.8 %all_to_all.20.t_ref = f32[16,8,384]{2,1,0:T(8,128)} all-to-all(f32[16,8,384]{2,1,0:T(8,128)S(1)} %terms.1), channel_id=1, replica_groups=mesh['grid'=16,'band'=8,'pole'=2] {'grid'}, dimensions={0} | all-to-all | bytes 393216 | tf_op jit(solution)/shard_map/all_to_all | solution.py:363
  63.3 2.1 %owner.1 = f32[16,8,128]{2,1,0:T(8,128)} custom-call(f32[16,8,384]{2,1,0:T(8,128)} %all_to_all.20.t_ref, f32[8,128]{1,0:T(8,128)} %coef_ref.1, s32[8,128]{1,0:T(8,128)} %atom_ref.1), custom_call_target="tpu_custom_call" | custom-call | tf_op jit(solution)/shard_map/owner/pallas_call | solution.py:365
  65.4 19.7 %all_to_all.21 = f32[16,8,128]{2,1,0:T(8,128)S(1)} all-to-all(f32[16,8,128]{2,1,0:T(8,128)} %owner.1), channel_id=1, replica_groups=mesh['grid'=16,'band'=8,'pole'=2] {'band','pole'}, dimensions={0} | all-to-all | bytes 131072 | tf_op jit(solution)/shard_map/all_to_all | solution.py:370
  85.1 0.6 slice_reduce_fusion
  (4 shorter events, 0.0 us)
Async XLA Ops:
  9.0 22.1 %all-to-all-start = ((bf16[16,16,512]{2,1,0:T(8,128)(2,1)}), bf16[16,16,512]{2,1,0:T(8,128)(2,1)S(1)}, u32[]{:S(2)}, u32[]{:S(2)}) async-start(bf16[16,16,512]{2,1,0:T(8,128)(2,1)} %get-tuple-element.11), calls=%async_computation | async-start | bytes 524288 | tf_op jit(solution)/shard_map/all_to_all | solution.py:305
  16.6 19.7 %collective-permute-start = (bf16[32,64,128]{2,1,0:T(8,128)(2,1)}, bf16[32,64,128]{2,1,0:T(8,128)(2,1)S(1)}, u32[]{:S(2)}, u32[]{:S(2)}) collective-permute-start(bf16[32,64,128]{2,1,0:T(8,128)(2,1)} %get-tuple-element.14), channel_id=1, source_target_pairs={{0,16},{16,32},{32,48},{48,64},{64,80},{80,96},{96,112},{112,128},... | collective-permute-start | bytes 1572872 | tf_op jit(solution)/shard_map/ppermute | solution.py:309
  18.0 18.4 %collective-permute-start.1 = (bf16[32,64,128]{2,1,0:T(8,128)(2,1)}, bf16[32,64,128]{2,1,0:T(8,128)(2,1)S(1)}, u32[]{:S(2)}, u32[]{:S(2)}) collective-permute-start(bf16[32,64,128]{2,1,0:T(8,128)(2,1)} %get-tuple-element.15), channel_id=1, source_target_pairs={{16,0},{32,16},{48,32},{64,48},{80,64},{96,80},{112,96},{128,112},... | collective-permute-start | bytes 1572872 | tf_op jit(solution)/shard_map/ppermute | solution.py:310
  21.5 9.6 %copy-start.2 = (s32[16,16]{1,0:T(8,128)S(1)}, s32[16,16]{1,0:T(8,128)}, u32[]{:S(2)}) copy-start(s32[16,16]{1,0:T(8,128)} %blk_ref.1) | copy-start | bytes 3076
  32.1 15.0 %all-to-all-start.1 = ((bf16[16,16,512]{2,1,0:T(8,128)(2,1)}), bf16[16,16,512]{2,1,0:T(8,128)(2,1)S(1)}, u32[]{:S(2)}, u32[]{:S(2)}) async-start(bf16[16,16,512]{2,1,0:T(8,128)(2,1)} %bitcast.3), calls=%async_computation.1 | async-start | bytes 524288 | tf_op jit(solution)/shard_map/all_to_all | solution.py:339
  36.3 10.9 %copy-start = (bf16[16,128,128]{2,1,0:T(8,128)(2,1)S(1)}, bf16[16,128,128]{2,1,0:T(8,128)(2,1)}, u32[]{:S(2)}) copy-start(bf16[16,128,128]{2,1,0:T(8,128)(2,1)} %inside.1.eyz_ref) | copy-start | bytes 1572868
  36.4 0.8 copy-start.3
  37.1 0.8 copy-start.4
  47.2 1.0 %copy-start.1 = (bf16[16,64,128]{2,1,0:T(8,128)(2,1)S(1)}, bf16[16,64,128]{2,1,0:T(8,128)(2,1)}, u32[]{:S(2)}) copy-start(bf16[16,64,128]{2,1,0:T(8,128)(2,1)} %across.1.ex_ref) | copy-start | bytes 786436

commit v3 on v2

--- a/solution.py
+++ b/solution.py
@@ -8,7 +8,7 @@
 ATOM_OWN = 56
 LANES = 128
 BF = jnp.bfloat16
-LIMIT = 57
+LIMIT = 24
 NY = 16
 GROUP = 8
 VALUE_GROUP = 4
@@ -266,7 +266,9 @@
     per_plane = rows // planes
     per = cols // bricks
     brick = lax.axis_index("grid").astype(jnp.int32)
-    x = solution.reshape(cols, planes, ny, nz)
+    x = pltpu.with_memory_space_constraint(solution.reshape(cols, planes, ny, nz), pltpu.HBM)
+    proj_vals = pltpu.with_memory_space_constraint(proj_vals, pltpu.HBM)
+    slot_offset = pltpu.with_memory_space_constraint(slot_offset, pltpu.HBM)
 
     def params(mib):
         return pltpu.CompilerParams(vmem_limit_bytes=mib << 20)

time: 86.2 us -> 78.9 us (0.915)
  Pallas kernels: 31.2 us -> 25.7 us
  waiting for transfers between devices: 0.01 us -> 3.07 us
  local copies, waits for them, and re-layouts: 2.61 us -> 0.08 us
  blocking collectives: 33.5 us -> 31.2 us
    pallas_call x1, Pallas kernels: 9.57 us -> 6.19 us  [forces(): pl.pallas_call(inside_kernel, out_shape=jax.ShapeDtypeStruct((slots, 2 *...]
    all_to_all x1, blocking collectives: 13.8 us -> 10.7 us  [forces(): at_owner = lax.all_to_all(terms, 'grid', 0, 0, tiled=True)]
    ppermute x1, waiting for transfers between devices: 0.01 us -> 3.06 us  [forces(): before = lax.ppermute(hi, 'grid', up)]
    unnamed x10 -> x2, local copies, waits for them, and re-layouts: 2.53 us -> 0.01 us
    pallas_call x1, Pallas kernels: 9.22 us -> 7.59 us  [forces(): pl.pallas_call(across_kernel, out_shape=jax.ShapeDtypeStruct((slots, cols...]
    all_to_all x1, blocking collectives: 19.7 us -> 20.6 us  [forces(): gathered = lax.all_to_all(shares, ('band', 'pole'), 0, 0, tiled=True)]
  transfers between devices with their start and end apart: 4 -> 4, of which waited for: 0 -> 1; matrix products, arithmetic and copies ran while one was open for 1% -> 1% of each run, Pallas kernels for 22% -> 18%
where the time goes in v3:
time: 78.9 us; the launch traced here: 78.4 us
  blocking collectives  31.2 us (40%)
  Pallas kernels  25.7 us (33%)
  starting transfers between devices  16 us (20%)
  waiting for transfers between devices  3.07 us (4%)
  matrix products  0.99 us (1%)
    all_to_all x1, blocking collectives, forces(): gathered = lax.all_to_all(shares, ('band', 'pole'), 0, 0, tiled=True)  20.6 us
    all_to_all x1, blocking collectives, forces(): at_owner = lax.all_to_all(terms, 'grid', 0, 0, tiled=True)  10.7 us
    pallas_call x1, Pallas kernels, forces(): pl.pallas_call(value_kernel, out_shape=(jax.ShapeDtypeStruct((rows, cols,...  8.54 us
    pallas_call x1, Pallas kernels, forces(): pl.pallas_call(across_kernel, out_shape=jax.ShapeDtypeStruct((slots, cols...  7.59 us
    all_to_all x1, starting transfers between devices, forces(): arrived = lax.all_to_all(c_part, 'grid', 0, 0, tiled=True)  7.58 us
    pallas_call x1, Pallas kernels, forces(): pl.pallas_call(inside_kernel, out_shape=jax.ShapeDtypeStruct((slots, 2 *...  6.19 us
    all_to_all x1, starting transfers between devices, forces(): lax.all_to_all(summed.reshape(bricks, slots, per * LANES), 'grid', 0, 0,...  3.53 us
    ppermute x1, starting transfers between devices, forces(): after = lax.ppermute(lo, 'grid', down)  3.5 us
  transfers between devices with their start and end apart: 4, of which 1 were waited for; matrix products, arithmetic and copies ran while one was open for 1% of the time, Pallas kernels for 18%

profile of v3, /device:TPU:1, one launch (start us, length us, event | category | flops | bytes accessed | tf_op | source)
XLA Modules:
  0.0 78.4 jit_solution(8902289869842487856)
XLA Ops:
  0.0 8.5 %values.1 = (bf16[128,64,128]{2,1,0:T(8,128)(2,1)S(1)}, bf16[32,64,128]{2,1,0:T(8,128)(2,1)}, bf16[32,64,128]{2,1,0:T(8,128)(2,1)}, bf16[16,16,512]{2,1,0:T(8,128)(2,1)}) custom-call(s32[16]{0:T(128)} %off_hbm.5, bf16[64,4,16,256]{3,2,1,0:T(8,128)(2,1)} %bitcast.5, bf16[16,128,2048]{2,1,0:T(8,128)(2,1)} %p_hbm.5), custom_call_target="tpu_custom_call" | custom-call | tf_op jit(solution)/shard_map/values/pallas_call | solution.py:281
  8.6 7.6 %all-to-all-start = ((bf16[16,16,512]{2,1,0:T(8,128)(2,1)}), bf16[16,16,512]{2,1,0:T(8,128)(2,1)S(1)}, u32[]{:S(2)}, u32[]{:S(2)}) async-start(bf16[16,16,512]{2,1,0:T(8,128)(2,1)} %get-tuple-element.11), calls=%async_computation | async-start | bytes 524288 | tf_op jit(solution)/shard_map/all_to_all | solution.py:307
  16.1 1.4 %collective-permute-start = (bf16[32,64,128]{2,1,0:T(8,128)(2,1)}, bf16[32,64,128]{2,1,0:T(8,128)(2,1)}, u32[]{:S(2)}, u32[]{:S(2)}) collective-permute-start(bf16[32,64,128]{2,1,0:T(8,128)(2,1)} %get-tuple-element.14), channel_id=1, source_target_pairs={{0,16},{16,32},{32,48},{48,64},{64,80},{80,96},{96,112},{112,128},... | collective-permute-start | bytes 1572872 | tf_op jit(solution)/shard_map/ppermute | solution.py:311
  17.5 3.5 %collective-permute-start.1 = (bf16[32,64,128]{2,1,0:T(8,128)(2,1)}, bf16[32,64,128]{2,1,0:T(8,128)(2,1)}, u32[]{:S(2)}, u32[]{:S(2)}) collective-permute-start(bf16[32,64,128]{2,1,0:T(8,128)(2,1)} %get-tuple-element.15), channel_id=1, source_target_pairs={{16,0},{32,16},{48,32},{64,48},{80,64},{96,80},{112,96},{128,112},... | collective-permute-start | bytes 1572872 | tf_op jit(solution)/shard_map/ppermute | solution.py:312
  21.0 0.0 copy-start
  21.0 6.2 %inside.1.eyz_ref = bf16[16,128,128]{2,1,0:T(8,128)(2,1)S(1)} custom-call(s32[16]{0:T(128)} %off_hbm.5, bf16[128,64,128]{2,1,0:T(8,128)(2,1)S(1)} %get-tuple-element.12.xr_hbm, bf16[16,128,2048]{2,1,0:T(8,128)(2,1)} %p_hbm.5), custom_call_target="tpu_custom_call" | custom-call | tf_op jit(solution)/shard_map/inside/pallas_call | solution.py:325
  27.2 0.0 copy-done
  27.2 0.1 eq.15
  27.3 0.0 all-to-all-done
  27.3 1.0 %convolution_convert_fusion = bf16[256,512]{1,0:T(8,128)(2,1)} fusion(bf16[256,512]{1,0:T(8,128)(2,1)S(1)} %bitcast.6, s32[256]{0:T(256)S(1)} %eq.15), kind=kOutput, calls=%fused_computation | convolution fusion | flops 67305472 | bytes 525312 | tf_op jit(solution)/shard_map/dot_general | solution.py:338
  28.3 3.5 %all-to-all-start.1 = ((bf16[16,16,512]{2,1,0:T(8,128)(2,1)}), bf16[16,16,512]{2,1,0:T(8,128)(2,1)S(1)}, u32[]{:S(2)}, u32[]{:S(2)}) async-start(bf16[16,16,512]{2,1,0:T(8,128)(2,1)} %bitcast.3), calls=%async_computation.1 | async-start | bytes 524288 | tf_op jit(solution)/shard_map/all_to_all | solution.py:341
  32.5 3.1 %collective-permute-done.before_ref = bf16[32,64,128]{2,1,0:T(8,128)(2,1)} collective-permute-done((bf16[32,64,128]{2,1,0:T(8,128)(2,1)}, bf16[32,64,128]{2,1,0:T(8,128)(2,1)}, u32[]{:S(2)}, u32[]{:S(2)}) %collective-permute-start) | collective-permute-done | bytes 524320 | tf_op jit(solution)/shard_map/ppermute | solution.py:311
  35.5 0.0 collective-permute-done.1.after_ref
  35.5 7.6 %across.1.ex_ref = bf16[16,64,128]{2,1,0:T(8,128)(2,1)S(1)} custom-call(s32[16]{0:T(128)} %off_hbm.5, bf16[128,64,128]{2,1,0:T(8,128)(2,1)S(1)} %get-tuple-element.12.xr_hbm, bf16[32,64,128]{2,1,0:T(8,128)(2,1)} %collective-permute-done.before_ref, bf16[32,64,128]{2,1,0:T(8,128)(2,1)} %collective-permute-done.1.after_ref, bf16[16,128,2048]{2,1,0:T(8,128)(2,1)} %p_hbm.5), custom_call_target="tpu_custom_call" | custom-call | tf_op jit(solution)/shard_map/across/pallas_call | solution.py:345
  43.1 0.0 all-to-all-done.1.c_ref
  43.1 1.3 %terms.1 = f32[16,8,384]{2,1,0:T(8,128)S(1)} custom-call(s32[16,16]{1,0:T(8,128)S(1)} %copy-done, s32[1]{0:T(128)} %bitcast.brick_ref, f32[1]{0:T(128)S(6)} %copy.8.w_ref, bf16[16,16,512]{2,1,0:T(8,128)(2,1)S(1)} %all-to-all-done.1.c_ref, bf16[16,64,128]{2,1,0:T(8,128)(2,1)S(1)} %across.1.ex_ref, bf16[16,128,128]{2,1,0:T(8,128)(2,1)S(1)} %inside.1.eyz_ref), custom_call_target="tpu_custom_call" | custom-call | tf_op jit(solution)/shard_map/terms/pallas_call | solution.py:355
  44.5 10.7 %all_to_all.20.t_ref = f32[16,8,384]{2,1,0:T(8,128)} all-to-all(f32[16,8,384]{2,1,0:T(8,128)S(1)} %terms.1), channel_id=1, replica_groups=mesh['grid'=16,'band'=8,'pole'=2] {'grid'}, dimensions={0} | all-to-all | bytes 393216 | tf_op jit(solution)/shard_map/all_to_all | solution.py:365
  55.1 2.1 %owner.1 = f32[16,8,128]{2,1,0:T(8,128)} custom-call(f32[16,8,384]{2,1,0:T(8,128)} %all_to_all.20.t_ref, f32[8,128]{1,0:T(8,128)} %coef_ref.1, s32[8,128]{1,0:T(8,128)} %atom_ref.1), custom_call_target="tpu_custom_call" | custom-call | tf_op jit(solution)/shard_map/owner/pallas_call | solution.py:367
  57.2 20.6 %all_to_all.21 = f32[16,8,128]{2,1,0:T(8,128)S(1)} all-to-all(f32[16,8,128]{2,1,0:T(8,128)} %owner.1), channel_id=1, replica_groups=mesh['grid'=16,'band'=8,'pole'=2] {'band','pole'}, dimensions={0} | all-to-all | bytes 131072 | tf_op jit(solution)/shard_map/all_to_all | solution.py:372
  77.8 0.6 slice_reduce_fusion
Async XLA Ops:
  8.6 18.7 %all-to-all-start = ((bf16[16,16,512]{2,1,0:T(8,128)(2,1)}), bf16[16,16,512]{2,1,0:T(8,128)(2,1)S(1)}, u32[]{:S(2)}, u32[]{:S(2)}) async-start(bf16[16,16,512]{2,1,0:T(8,128)(2,1)} %get-tuple-element.11), calls=%async_computation | async-start | bytes 524288 | tf_op jit(solution)/shard_map/all_to_all | solution.py:307
  16.1 19.4 %collective-permute-start = (bf16[32,64,128]{2,1,0:T(8,128)(2,1)}, bf16[32,64,128]{2,1,0:T(8,128)(2,1)}, u32[]{:S(2)}, u32[]{:S(2)}) collective-permute-start(bf16[32,64,128]{2,1,0:T(8,128)(2,1)} %get-tuple-element.14), channel_id=1, source_target_pairs={{0,16},{16,32},{32,48},{48,64},{64,80},{80,96},{96,112},{112,128},... | collective-permute-start | bytes 1572872 | tf_op jit(solution)/shard_map/ppermute | solution.py:311
  17.5 18.0 %collective-permute-start.1 = (bf16[32,64,128]{2,1,0:T(8,128)(2,1)}, bf16[32,64,128]{2,1,0:T(8,128)(2,1)}, u32[]{:S(2)}, u32[]{:S(2)}) collective-permute-start(bf16[32,64,128]{2,1,0:T(8,128)(2,1)} %get-tuple-element.15), channel_id=1, source_target_pairs={{16,0},{32,16},{48,32},{64,48},{80,64},{96,80},{112,96},{128,112},... | collective-permute-start | bytes 1572872 | tf_op jit(solution)/shard_map/ppermute | solution.py:312
  21.0 6.2 %copy-start = (s32[16,16]{1,0:T(8,128)S(1)}, s32[16,16]{1,0:T(8,128)}, u32[]{:S(2)}) copy-start(s32[16,16]{1,0:T(8,128)} %blk_ref.1) | copy-start | bytes 3076
  28.3 14.9 %all-to-all-start.1 = ((bf16[16,16,512]{2,1,0:T(8,128)(2,1)}), bf16[16,16,512]{2,1,0:T(8,128)(2,1)S(1)}, u32[]{:S(2)}, u32[]{:S(2)}) async-start(bf16[16,16,512]{2,1,0:T(8,128)(2,1)} %bitcast.3), calls=%async_computation.1 | async-start | bytes 524288 | tf_op jit(solution)/shard_map/all_to_all | solution.py:341

commit v4 on v3

--- a/solution.py
+++ b/solution.py
@@ -10,7 +10,7 @@
 BF = jnp.bfloat16
 LIMIT = 24
 NY = 16
-GROUP = 8
+GROUP = 4
 VALUE_GROUP = 4
 AHEAD = 8
 GROUP_COLS = 16
@@ -208,7 +208,7 @@
     partials(off, p_hbm, pbuf, psem, fields, e_ref)
 
 
-def term_kernel(blk_ref, brick_ref, w_ref, c_ref, ex_ref, eyz_ref, t_ref, c32):
+def term_kernel(blk_ref, brick_ref, w_ref, c_ref, ex_ref, eyz_ref, out_ref, c32, t_ref):
     dests, slots, _ = c_ref.shape
     cols = ex_ref.shape[1]
     per = cols // dests
@@ -230,29 +230,30 @@
             term = jnp.sum(c * parts[x].astype(F32), axis=0, keepdims=True)
             at = slice(x * LANES, (x + 1) * LANES)
             t_ref[o, :, at] = t_ref[o, :, at] + jnp.where(here, term, 0.0)
+    out_ref[...] = t_ref[...].astype(BF)
 
 
 def owner_kernel(t_ref, coef_ref, atom_ref, out_ref):
     owned = coef_ref.shape[0]
     scale = -coef_ref[...]
+    total = t_ref[0].astype(F32)
+    for s in range(1, t_ref.shape[0]):
+        total = total + t_ref[s].astype(F32)
+    row = lax.broadcasted_iota(jnp.int32, (8, LANES), 0)
     atom_id = lax.broadcasted_iota(jnp.int32, (LANES, LANES), 0)
-    total = t_ref[0]
-    for s in range(1, t_ref.shape[0]):
-        total = total + t_ref[s]
-    hits = [atom_ref[b : b + 1, :] == atom_id for b in range(owned)]
-    row = lax.broadcasted_iota(jnp.int32, (8, LANES), 0)
-    ones = jnp.ones((8, LANES), F32)
-    out = jnp.zeros((8, LANES), F32)
-    for x in range(3):
-        terms = total[:, x * LANES : (x + 1) * LANES] * scale
-        acc = jnp.zeros((LANES, LANES), F32)
-        for b in range(owned):
-            acc = acc + jnp.where(hits[b], terms[b : b + 1, :], 0.0)
-        sums = lax.dot_general(
-            ones, acc, (((1,), (1,)), ((), ())),
-            preferred_element_type=F32, precision=lax.Precision.HIGHEST,
-        )
-        out = jnp.where(row == x, sums, out)
+    terms = [total[:, x * LANES : (x + 1) * LANES] * scale for x in range(3)]
+    values, hits = [], []
+    for b in range(owned):
+        value = jnp.zeros((8, LANES), F32)
+        for x in range(3):
+            value = jnp.where(row == x, terms[x][b : b + 1], value)
+        values.append(value)
+        hits.append(jnp.where(atom_ref[b : b + 1, :] == atom_id, 1.0, 0.0).astype(BF))
+    value = jnp.concatenate(values, axis=1)
+    high = value.astype(BF)
+    low = (value - high.astype(F32)).astype(BF)
+    sums = contract(jnp.concatenate([high, low], axis=0), jnp.concatenate(hits, axis=1))
+    out = sums[:8] + sums[8:]
     for d in range(out_ref.shape[0]):
         out_ref[d] = out
 
@@ -354,10 +355,13 @@
 
     terms = pl.pallas_call(
         term_kernel,
-        out_shape=jax.ShapeDtypeStruct((bricks, owned, 3 * LANES), F32),
+        out_shape=jax.ShapeDtypeStruct((bricks, owned, 3 * LANES), BF),
         in_specs=[smem, smem, smem, vmem, vmem, vmem],
         out_specs=vmem,
-        scratch_shapes=[pltpu.VMEM((slots * cols, LANES), F32)],
+        scratch_shapes=[
+            pltpu.VMEM((slots * cols, LANES), F32),
+            pltpu.VMEM((bricks, owned, 3 * LANES), F32),
+        ],
         compiler_params=params(8),
         name="terms",
     )(slot_block, brick[None], pole_weight, coefs, e_x, e_yz)
@@ -367,6 +371,7 @@
     shares = pl.pallas_call(
         owner_kernel,
         out_shape=jax.ShapeDtypeStruct((copies, 8, LANES), F32),
+        compiler_params=params(4),
         name="owner",
     )(at_owner, proj_coef, proj_atom)
     gathered = lax.all_to_all(shares, ("band", "pole"), 0, 0, tiled=True)

time: 78.9 us -> 75.6 us (0.958)
  Pallas kernels: 25.7 us -> 23.1 us
  blocking collectives: 31.2 us -> 30.4 us
    pallas_call x1, Pallas kernels: 2.09 us -> 0.22 us  [forces(): pl.pallas_call(owner_kernel, out_shape=jax.ShapeDtypeStruct((copies, 8, L...]
    all_to_all x1, blocking collectives: 10.7 us -> 9.85 us  [forces(): at_owner = lax.all_to_all(terms, 'grid', 0, 0, tiled=True)]
  transfers between devices with their start and end apart: 4 -> 4, of which waited for: 1 -> 1; matrix products, arithmetic and copies ran while one was open for 1% -> 1% of each run, Pallas kernels for 18% -> 17%
where the time goes in v4:
time: 75.6 us; the launch traced here: 75.2 us
  blocking collectives  30.4 us (40%)
  Pallas kernels  23.1 us (31%)
  starting transfers between devices  16 us (21%)
  waiting for transfers between devices  3.24 us (4%)
  matrix products  0.98 us (1%)
    all_to_all x1, blocking collectives, forces(): gathered = lax.all_to_all(shares, ('band', 'pole'), 0, 0, tiled=True)  20.6 us
    all_to_all x1, blocking collectives, forces(): at_owner = lax.all_to_all(terms, 'grid', 0, 0, tiled=True)  9.85 us
    pallas_call x1, Pallas kernels, forces(): pl.pallas_call(value_kernel, out_shape=(jax.ShapeDtypeStruct((rows, cols,...  8.53 us
    all_to_all x1, starting transfers between devices, forces(): arrived = lax.all_to_all(c_part, 'grid', 0, 0, tiled=True)  7.58 us
    pallas_call x1, Pallas kernels, forces(): pl.pallas_call(across_kernel, out_shape=jax.ShapeDtypeStruct((slots, cols...  7.01 us
    pallas_call x1, Pallas kernels, forces(): pl.pallas_call(inside_kernel, out_shape=jax.ShapeDtypeStruct((slots, 2 *...  6.01 us
    all_to_all x1, starting transfers between devices, forces(): lax.all_to_all(summed.reshape(bricks, slots, per * LANES), 'grid', 0, 0,...  3.53 us
    ppermute x1, starting transfers between devices, forces(): after = lax.ppermute(lo, 'grid', down)  3.5 us
  transfers between devices with their start and end apart: 4, of which 1 were waited for; matrix products, arithmetic and copies ran while one was open for 1% of the time, Pallas kernels for 17%

profile of v4, /device:TPU:1, one launch (start us, length us, event | category | flops | bytes accessed | tf_op | source)
XLA Modules:
  0.0 75.2 jit_solution(4723295105183659692)
XLA Ops:
  0.0 8.5 %values.1 = (bf16[128,64,128]{2,1,0:T(8,128)(2,1)S(1)}, bf16[32,64,128]{2,1,0:T(8,128)(2,1)}, bf16[32,64,128]{2,1,0:T(8,128)(2,1)}, bf16[16,16,512]{2,1,0:T(8,128)(2,1)}) custom-call(s32[16]{0:T(128)} %off_hbm.5, bf16[64,4,16,256]{3,2,1,0:T(8,128)(2,1)} %bitcast.5, bf16[16,128,2048]{2,1,0:T(8,128)(2,1)} %p_hbm.5), custom_call_target="tpu_custom_call" | custom-call | tf_op jit(solution)/shard_map/values/pallas_call | solution.py:282
  8.5 7.6 %all-to-all-start = ((bf16[16,16,512]{2,1,0:T(8,128)(2,1)}), bf16[16,16,512]{2,1,0:T(8,128)(2,1)S(1)}, u32[]{:S(2)}, u32[]{:S(2)}) async-start(bf16[16,16,512]{2,1,0:T(8,128)(2,1)} %get-tuple-element.11), calls=%async_computation | async-start | bytes 524288 | tf_op jit(solution)/shard_map/all_to_all | solution.py:308
  16.1 1.4 %collective-permute-start = (bf16[32,64,128]{2,1,0:T(8,128)(2,1)}, bf16[32,64,128]{2,1,0:T(8,128)(2,1)}, u32[]{:S(2)}, u32[]{:S(2)}) collective-permute-start(bf16[32,64,128]{2,1,0:T(8,128)(2,1)} %get-tuple-element.14), channel_id=1, source_target_pairs={{0,16},{16,32},{32,48},{48,64},{64,80},{80,96},{96,112},{112,128},... | collective-permute-start | bytes 1572872 | tf_op jit(solution)/shard_map/ppermute | solution.py:312
  17.5 3.5 %collective-permute-start.1 = (bf16[32,64,128]{2,1,0:T(8,128)(2,1)}, bf16[32,64,128]{2,1,0:T(8,128)(2,1)}, u32[]{:S(2)}, u32[]{:S(2)}) collective-permute-start(bf16[32,64,128]{2,1,0:T(8,128)(2,1)} %get-tuple-element.15), channel_id=1, source_target_pairs={{16,0},{32,16},{48,32},{64,48},{80,64},{96,80},{112,96},{128,112},... | collective-permute-start | bytes 1572872 | tf_op jit(solution)/shard_map/ppermute | solution.py:313
  21.0 0.0 copy-start
  21.0 6.0 %inside.1.eyz_ref = bf16[16,128,128]{2,1,0:T(8,128)(2,1)S(1)} custom-call(s32[16]{0:T(128)} %off_hbm.5, bf16[128,64,128]{2,1,0:T(8,128)(2,1)S(1)} %get-tuple-element.12.xr_hbm, bf16[16,128,2048]{2,1,0:T(8,128)(2,1)} %p_hbm.5), custom_call_target="tpu_custom_call" | custom-call | tf_op jit(solution)/shard_map/inside/pallas_call | solution.py:326
  27.0 0.0 copy-done
  27.0 0.1 eq.15
  27.1 0.0 all-to-all-done
  27.1 1.0 %convolution_convert_fusion = bf16[256,512]{1,0:T(8,128)(2,1)} fusion(bf16[256,512]{1,0:T(8,128)(2,1)S(1)} %bitcast.6, s32[256]{0:T(256)S(1)} %eq.15), kind=kOutput, calls=%fused_computation | convolution fusion | flops 67305472 | bytes 525312 | tf_op jit(solution)/shard_map/dot_general | solution.py:339
  28.1 3.5 %all-to-all-start.1 = ((bf16[16,16,512]{2,1,0:T(8,128)(2,1)}), bf16[16,16,512]{2,1,0:T(8,128)(2,1)S(1)}, u32[]{:S(2)}, u32[]{:S(2)}) async-start(bf16[16,16,512]{2,1,0:T(8,128)(2,1)} %bitcast.3), calls=%async_computation.1 | async-start | bytes 524288 | tf_op jit(solution)/shard_map/all_to_all | solution.py:342
  32.3 0.0 copy-start.1
  32.3 0.0 copy-start.2
  32.3 3.2 %collective-permute-done.before_ref = bf16[32,64,128]{2,1,0:T(8,128)(2,1)} collective-permute-done((bf16[32,64,128]{2,1,0:T(8,128)(2,1)}, bf16[32,64,128]{2,1,0:T(8,128)(2,1)}, u32[]{:S(2)}, u32[]{:S(2)}) %collective-permute-start) | collective-permute-done | bytes 524320 | tf_op jit(solution)/shard_map/ppermute | solution.py:312
  35.5 0.0 collective-permute-done.1.after_ref
  35.5 7.0 %across.1.ex_ref = bf16[16,64,128]{2,1,0:T(8,128)(2,1)S(1)} custom-call(s32[16]{0:T(128)} %off_hbm.5, bf16[128,64,128]{2,1,0:T(8,128)(2,1)S(1)} %get-tuple-element.12.xr_hbm, bf16[32,64,128]{2,1,0:T(8,128)(2,1)} %collective-permute-done.before_ref, bf16[32,64,128]{2,1,0:T(8,128)(2,1)} %collective-permute-done.1.after_ref, bf16[16,128,2048]{2,1,0:T(8,128)(2,1)} %p_hbm.5), custom_call_target="tpu_custom_call" | custom-call | tf_op jit(solution)/shard_map/across/pallas_call | solution.py:346
  42.5 0.0 all-to-all-done.1.c_ref
  42.6 1.4 %terms.1 = bf16[16,8,384]{2,1,0:T(8,128)(2,1)S(1)} custom-call(s32[16,16]{1,0:T(8,128)S(1)} %copy-done, s32[1]{0:T(128)} %bitcast.brick_ref, f32[1]{0:T(128)S(6)} %copy.8.w_ref, bf16[16,16,512]{2,1,0:T(8,128)(2,1)S(1)} %all-to-all-done.1.c_ref, bf16[16,64,128]{2,1,0:T(8,128)(2,1)S(1)} %across.1.ex_ref, bf16[16,128,128]{2,1,0:T(8,128)(2,1)S(1)} %inside.1.eyz_ref), custom_call_target="tpu_custom_call" | custom-call | tf_op jit(solution)/shard_map/terms/pallas_call | solution.py:356
  43.9 9.8 %all_to_all.20.t_ref = bf16[16,8,384]{2,1,0:T(8,128)(2,1)S(1)} all-to-all(bf16[16,8,384]{2,1,0:T(8,128)(2,1)S(1)} %terms.1), channel_id=1, replica_groups=mesh['grid'=16,'band'=8,'pole'=2] {'grid'}, dimensions={0} | all-to-all | bytes 196608 | tf_op jit(solution)/shard_map/all_to_all | solution.py:369
  53.8 0.0 copy-done.1
  53.8 0.0 copy-done.2
  53.8 0.2 owner.1
  54.0 20.6 %all_to_all.21 = f32[16,8,128]{2,1,0:T(8,128)S(1)} all-to-all(f32[16,8,128]{2,1,0:T(8,128)S(1)} %owner.1), channel_id=1, replica_groups=mesh['grid'=16,'band'=8,'pole'=2] {'band','pole'}, dimensions={0} | all-to-all | bytes 131072 | tf_op jit(solution)/shard_map/all_to_all | solution.py:377
  74.6 0.6 slice_reduce_fusion
Async XLA Ops:
  8.5 18.6 %all-to-all-start = ((bf16[16,16,512]{2,1,0:T(8,128)(2,1)}), bf16[16,16,512]{2,1,0:T(8,128)(2,1)S(1)}, u32[]{:S(2)}, u32[]{:S(2)}) async-start(bf16[16,16,512]{2,1,0:T(8,128)(2,1)} %get-tuple-element.11), calls=%async_computation | async-start | bytes 524288 | tf_op jit(solution)/shard_map/all_to_all | solution.py:308
  16.1 19.4 %collective-permute-start = (bf16[32,64,128]{2,1,0:T(8,128)(2,1)}, bf16[32,64,128]{2,1,0:T(8,128)(2,1)}, u32[]{:S(2)}, u32[]{:S(2)}) collective-permute-start(bf16[32,64,128]{2,1,0:T(8,128)(2,1)} %get-tuple-element.14), channel_id=1, source_target_pairs={{0,16},{16,32},{32,48},{48,64},{64,80},{80,96},{96,112},{112,128},... | collective-permute-start | bytes 1572872 | tf_op jit(solution)/shard_map/ppermute | solution.py:312
  17.5 18.0 %collective-permute-start.1 = (bf16[32,64,128]{2,1,0:T(8,128)(2,1)}, bf16[32,64,128]{2,1,0:T(8,128)(2,1)}, u32[]{:S(2)}, u32[]{:S(2)}) collective-permute-start(bf16[32,64,128]{2,1,0:T(8,128)(2,1)} %get-tuple-element.15), channel_id=1, source_target_pairs={{16,0},{32,16},{48,32},{64,48},{80,64},{96,80},{112,96},{128,112},... | collective-permute-start | bytes 1572872 | tf_op jit(solution)/shard_map/ppermute | solution.py:313
  21.0 6.0 %copy-start = (s32[16,16]{1,0:T(8,128)S(1)}, s32[16,16]{1,0:T(8,128)}, u32[]{:S(2)}) copy-start(s32[16,16]{1,0:T(8,128)} %blk_ref.1) | copy-start | bytes 3076
  28.1 14.5 %all-to-all-start.1 = ((bf16[16,16,512]{2,1,0:T(8,128)(2,1)}), bf16[16,16,512]{2,1,0:T(8,128)(2,1)S(1)}, u32[]{:S(2)}, u32[]{:S(2)}) async-start(bf16[16,16,512]{2,1,0:T(8,128)(2,1)} %bitcast.3), calls=%async_computation.1 | async-start | bytes 524288 | tf_op jit(solution)/shard_map/all_to_all | solution.py:342
  32.3 21.5 %copy-start.1 = (f32[8,128]{1,0:T(8,128)S(1)}, f32[8,128]{1,0:T(8,128)}, u32[]{:S(2)}) copy-start(f32[8,128]{1,0:T(8,128)} %coef_ref.1) | copy-start | bytes 12292
  32.3 21.5 %copy-start.2 = (s32[8,128]{1,0:T(8,128)S(1)}, s32[8,128]{1,0:T(8,128)}, u32[]{:S(2)}) copy-start(s32[8,128]{1,0:T(8,128)} %atom_ref.1) | copy-start | bytes 12292

commit v5 on v4

--- a/solution.py
+++ b/solution.py
@@ -12,7 +12,7 @@
 NY = 16
 GROUP = 4
 VALUE_GROUP = 4
-AHEAD = 8
+AHEAD = 12
 GROUP_COLS = 16
 F32 = jnp.float32
 
@@ -65,8 +65,6 @@
         x_copy(g).start()
     off_copy = pltpu.make_async_copy(off_hbm, off, osem)
     off_copy.start()
-    for k in range(AHEAD):
-        p_copy(k).start()
     outgoing = [
         pltpu.make_async_copy(xr, xr_hbm, rsem.at[0]),
         pltpu.make_async_copy(xr.at[plane(0)], lo_hbm, rsem.at[1]),
@@ -74,6 +72,8 @@
     ]
     for g in range(cols // GROUP_COLS):
         x_copy(g).wait()
+        for k in range(g * slots * GROUP_COLS // cols, (g + 1) * slots * GROUP_COLS // cols):
+            p_copy(k).start()
         part = slice(g * GROUP_COLS, (g + 1) * GROUP_COLS)
         for x in range(planes):
             for half in range(halves):
@@ -89,11 +89,6 @@
     def group(i, carry):
         for u in range(VALUE_GROUP):
             p_copy(i * VALUE_GROUP + u).wait()
-
-        @pl.when(i * VALUE_GROUP + AHEAD < slots)
-        def _():
-            for u in range(VALUE_GROUP):
-                p_copy(i * VALUE_GROUP + u + AHEAD).start()
 
         for u in range(VALUE_GROUP):
             k = i * VALUE_GROUP + u

time: 75.6 us -> 75 us (level)
  no operation moved by 1% of the time
where the time goes in v5:
time: 75 us; the launch traced here: 74.5 us
  blocking collectives  30.4 us (41%)
  Pallas kernels  22.5 us (30%)
  starting transfers between devices  16 us (21%)
  waiting for transfers between devices  3.24 us (4%)
  matrix products  0.98 us (1%)
    all_to_all x1, blocking collectives, forces(): gathered = lax.all_to_all(shares, ('band', 'pole'), 0, 0, tiled=True)  20.6 us
    all_to_all x1, blocking collectives, forces(): at_owner = lax.all_to_all(terms, 'grid', 0, 0, tiled=True)  9.85 us
    pallas_call x1, Pallas kernels, forces(): pl.pallas_call(value_kernel, out_shape=(jax.ShapeDtypeStruct((rows, cols,...  7.89 us
    all_to_all x1, starting transfers between devices, forces(): arrived = lax.all_to_all(c_part, 'grid', 0, 0, tiled=True)  7.59 us
    pallas_call x1, Pallas kernels, forces(): pl.pallas_call(across_kernel, out_shape=jax.ShapeDtypeStruct((slots, cols...  7.01 us
    pallas_call x1, Pallas kernels, forces(): pl.pallas_call(inside_kernel, out_shape=jax.ShapeDtypeStruct((slots, 2 *...  6.01 us
    all_to_all x1, starting transfers between devices, forces(): lax.all_to_all(summed.reshape(bricks, slots, per * LANES), 'grid', 0, 0,...  3.53 us
    ppermute x1, starting transfers between devices, forces(): after = lax.ppermute(lo, 'grid', down)  3.5 us
  transfers between devices with their start and end apart: 4, of which 1 were waited for; matrix products, arithmetic and copies ran while one was open for 1% of the time, Pallas kernels for 17%

profile of v5, /device:TPU:1, one launch (start us, length us, event | category | flops | bytes accessed | tf_op | source)
XLA Modules:
  0.0 74.5 jit_solution(9385114181422555470)
XLA Ops:
  0.0 7.9 %values.1 = (bf16[128,64,128]{2,1,0:T(8,128)(2,1)S(1)}, bf16[32,64,128]{2,1,0:T(8,128)(2,1)}, bf16[32,64,128]{2,1,0:T(8,128)(2,1)}, bf16[16,16,512]{2,1,0:T(8,128)(2,1)}) custom-call(s32[16]{0:T(128)} %off_hbm.5, bf16[64,4,16,256]{3,2,1,0:T(8,128)(2,1)} %bitcast.5, bf16[16,128,2048]{2,1,0:T(8,128)(2,1)} %p_hbm.5), custom_call_target="tpu_custom_call" | custom-call | tf_op jit(solution)/shard_map/values/pallas_call | solution.py:277
  7.9 7.6 %all-to-all-start = ((bf16[16,16,512]{2,1,0:T(8,128)(2,1)}), bf16[16,16,512]{2,1,0:T(8,128)(2,1)S(1)}, u32[]{:S(2)}, u32[]{:S(2)}) async-start(bf16[16,16,512]{2,1,0:T(8,128)(2,1)} %get-tuple-element.11), calls=%async_computation | async-start | bytes 524288 | tf_op jit(solution)/shard_map/all_to_all | solution.py:303
  15.5 1.4 %collective-permute-start = (bf16[32,64,128]{2,1,0:T(8,128)(2,1)}, bf16[32,64,128]{2,1,0:T(8,128)(2,1)}, u32[]{:S(2)}, u32[]{:S(2)}) collective-permute-start(bf16[32,64,128]{2,1,0:T(8,128)(2,1)} %get-tuple-element.14), channel_id=1, source_target_pairs={{0,16},{16,32},{32,48},{48,64},{64,80},{80,96},{96,112},{112,128},... | collective-permute-start | bytes 1572872 | tf_op jit(solution)/shard_map/ppermute | solution.py:307
  16.9 3.5 %collective-permute-start.1 = (bf16[32,64,128]{2,1,0:T(8,128)(2,1)}, bf16[32,64,128]{2,1,0:T(8,128)(2,1)}, u32[]{:S(2)}, u32[]{:S(2)}) collective-permute-start(bf16[32,64,128]{2,1,0:T(8,128)(2,1)} %get-tuple-element.15), channel_id=1, source_target_pairs={{16,0},{32,16},{48,32},{64,48},{80,64},{96,80},{112,96},{128,112},... | collective-permute-start | bytes 1572872 | tf_op jit(solution)/shard_map/ppermute | solution.py:308
  20.4 0.0 copy-start
  20.4 6.0 %inside.1.eyz_ref = bf16[16,128,128]{2,1,0:T(8,128)(2,1)S(1)} custom-call(s32[16]{0:T(128)} %off_hbm.5, bf16[128,64,128]{2,1,0:T(8,128)(2,1)S(1)} %get-tuple-element.12.xr_hbm, bf16[16,128,2048]{2,1,0:T(8,128)(2,1)} %p_hbm.5), custom_call_target="tpu_custom_call" | custom-call | tf_op jit(solution)/shard_map/inside/pallas_call | solution.py:321
  26.4 0.0 copy-done
  26.4 0.1 eq.15
  26.5 0.0 all-to-all-done
  26.5 1.0 %convolution_convert_fusion = bf16[256,512]{1,0:T(8,128)(2,1)} fusion(bf16[256,512]{1,0:T(8,128)(2,1)S(1)} %bitcast.6, s32[256]{0:T(256)S(1)} %eq.15), kind=kOutput, calls=%fused_computation | convolution fusion | flops 67305472 | bytes 525312 | tf_op jit(solution)/shard_map/dot_general | solution.py:334
  27.4 3.5 %all-to-all-start.1 = ((bf16[16,16,512]{2,1,0:T(8,128)(2,1)}), bf16[16,16,512]{2,1,0:T(8,128)(2,1)S(1)}, u32[]{:S(2)}, u32[]{:S(2)}) async-start(bf16[16,16,512]{2,1,0:T(8,128)(2,1)} %bitcast.3), calls=%async_computation.1 | async-start | bytes 524288 | tf_op jit(solution)/shard_map/all_to_all | solution.py:337
  31.6 0.0 copy-start.1
  31.7 0.0 copy-start.2
  31.7 3.2 %collective-permute-done.before_ref = bf16[32,64,128]{2,1,0:T(8,128)(2,1)} collective-permute-done((bf16[32,64,128]{2,1,0:T(8,128)(2,1)}, bf16[32,64,128]{2,1,0:T(8,128)(2,1)}, u32[]{:S(2)}, u32[]{:S(2)}) %collective-permute-start) | collective-permute-done | bytes 524320 | tf_op jit(solution)/shard_map/ppermute | solution.py:307
  34.9 0.0 collective-permute-done.1.after_ref
  34.9 7.0 %across.1.ex_ref = bf16[16,64,128]{2,1,0:T(8,128)(2,1)S(1)} custom-call(s32[16]{0:T(128)} %off_hbm.5, bf16[128,64,128]{2,1,0:T(8,128)(2,1)S(1)} %get-tuple-element.12.xr_hbm, bf16[32,64,128]{2,1,0:T(8,128)(2,1)} %collective-permute-done.before_ref, bf16[32,64,128]{2,1,0:T(8,128)(2,1)} %collective-permute-done.1.after_ref, bf16[16,128,2048]{2,1,0:T(8,128)(2,1)} %p_hbm.5), custom_call_target="tpu_custom_call" | custom-call | tf_op jit(solution)/shard_map/across/pallas_call | solution.py:341
  41.9 0.0 all-to-all-done.1.c_ref
  41.9 1.4 %terms.1 = bf16[16,8,384]{2,1,0:T(8,128)(2,1)S(1)} custom-call(s32[16,16]{1,0:T(8,128)S(1)} %copy-done, s32[1]{0:T(128)} %bitcast.brick_ref, f32[1]{0:T(128)S(6)} %copy.8.w_ref, bf16[16,16,512]{2,1,0:T(8,128)(2,1)S(1)} %all-to-all-done.1.c_ref, bf16[16,64,128]{2,1,0:T(8,128)(2,1)S(1)} %across.1.ex_ref, bf16[16,128,128]{2,1,0:T(8,128)(2,1)S(1)} %inside.1.eyz_ref), custom_call_target="tpu_custom_call" | custom-call | tf_op jit(solution)/shard_map/terms/pallas_call | solution.py:351
  43.3 9.8 %all_to_all.20.t_ref = bf16[16,8,384]{2,1,0:T(8,128)(2,1)S(1)} all-to-all(bf16[16,8,384]{2,1,0:T(8,128)(2,1)S(1)} %terms.1), channel_id=1, replica_groups=mesh['grid'=16,'band'=8,'pole'=2] {'grid'}, dimensions={0} | all-to-all | bytes 196608 | tf_op jit(solution)/shard_map/all_to_all | solution.py:364
  53.1 0.0 copy-done.1
  53.1 0.0 copy-done.2
  53.1 0.2 owner.1
  53.3 20.6 %all_to_all.21 = f32[16,8,128]{2,1,0:T(8,128)S(1)} all-to-all(f32[16,8,128]{2,1,0:T(8,128)S(1)} %owner.1), channel_id=1, replica_groups=mesh['grid'=16,'band'=8,'pole'=2] {'band','pole'}, dimensions={0} | all-to-all | bytes 131072 | tf_op jit(solution)/shard_map/all_to_all | solution.py:372
  73.9 0.6 slice_reduce_fusion
Async XLA Ops:
  7.9 18.6 %all-to-all-start = ((bf16[16,16,512]{2,1,0:T(8,128)(2,1)}), bf16[16,16,512]{2,1,0:T(8,128)(2,1)S(1)}, u32[]{:S(2)}, u32[]{:S(2)}) async-start(bf16[16,16,512]{2,1,0:T(8,128)(2,1)} %get-tuple-element.11), calls=%async_computation | async-start | bytes 524288 | tf_op jit(solution)/shard_map/all_to_all | solution.py:303
  15.5 19.4 %collective-permute-start = (bf16[32,64,128]{2,1,0:T(8,128)(2,1)}, bf16[32,64,128]{2,1,0:T(8,128)(2,1)}, u32[]{:S(2)}, u32[]{:S(2)}) collective-permute-start(bf16[32,64,128]{2,1,0:T(8,128)(2,1)} %get-tuple-element.14), channel_id=1, source_target_pairs={{0,16},{16,32},{32,48},{48,64},{64,80},{80,96},{96,112},{112,128},... | collective-permute-start | bytes 1572872 | tf_op jit(solution)/shard_map/ppermute | solution.py:307
  16.9 18.0 %collective-permute-start.1 = (bf16[32,64,128]{2,1,0:T(8,128)(2,1)}, bf16[32,64,128]{2,1,0:T(8,128)(2,1)}, u32[]{:S(2)}, u32[]{:S(2)}) collective-permute-start(bf16[32,64,128]{2,1,0:T(8,128)(2,1)} %get-tuple-element.15), channel_id=1, source_target_pairs={{16,0},{32,16},{48,32},{64,48},{80,64},{96,80},{112,96},{128,112},... | collective-permute-start | bytes 1572872 | tf_op jit(solution)/shard_map/ppermute | solution.py:308
  20.4 6.0 %copy-start = (s32[16,16]{1,0:T(8,128)S(1)}, s32[16,16]{1,0:T(8,128)}, u32[]{:S(2)}) copy-start(s32[16,16]{1,0:T(8,128)} %blk_ref.1) | copy-start | bytes 3076
  27.4 14.5 %all-to-all-start.1 = ((bf16[16,16,512]{2,1,0:T(8,128)(2,1)}), bf16[16,16,512]{2,1,0:T(8,128)(2,1)S(1)}, u32[]{:S(2)}, u32[]{:S(2)}) async-start(bf16[16,16,512]{2,1,0:T(8,128)(2,1)} %bitcast.3), calls=%async_computation.1 | async-start | bytes 524288 | tf_op jit(solution)/shard_map/all_to_all | solution.py:337
  31.6 21.5 %copy-start.1 = (f32[8,128]{1,0:T(8,128)S(1)}, f32[8,128]{1,0:T(8,128)}, u32[]{:S(2)}) copy-start(f32[8,128]{1,0:T(8,128)} %coef_ref.1) | copy-start | bytes 12292
  31.7 21.5 %copy-start.2 = (s32[8,128]{1,0:T(8,128)S(1)}, s32[8,128]{1,0:T(8,128)}, u32[]{:S(2)}) copy-start(s32[8,128]{1,0:T(8,128)} %atom_ref.1) | copy-start | bytes 12292

commit v6 on v5

--- a/solution.py
+++ b/solution.py
@@ -145,10 +145,8 @@
     lax.fori_loop(0, slots // GROUP, group, 0)
 
 
-def inside_kernel(off_hbm, xr_hbm, p_hbm, e_ref, off, xr, fields, pbuf, osem, xsem, psem):
+def inside_kernel(off_hbm, xr, p_hbm, e_ref, off, fields, pbuf, osem, psem):
     rows, cols, _ = xr.shape
-    xr_copy = pltpu.make_async_copy(xr_hbm, xr, xsem)
-    xr_copy.start()
     offsets = fetch_blocks(off_hbm, off, p_hbm, pbuf, osem, psem)
     lane = lax.broadcasted_iota(jnp.int32, (cols, LANES), 1)
     last = lane == LANES - 1
@@ -171,19 +169,16 @@
         fields[h + 1, cols:] = jnp.where(last, a_up, b_up) - jnp.where(first, a_down, b_down)
         return carry
 
-    xr_copy.wait()
     lax.fori_loop(0, rows // 2, pair, 0, unroll=4)
     offsets.wait()
     partials(off, p_hbm, pbuf, psem, fields, e_ref)
 
 
 def across_kernel(
-    off_hbm, xr_hbm, before_ref, after_ref, p_hbm, e_ref, off, xr, fields, pbuf, osem, xsem, psem
+    off_hbm, xr, before_ref, after_ref, p_hbm, e_ref, off, fields, pbuf, osem, psem
 ):
     rows = xr.shape[0]
     per_plane = before_ref.shape[0]
-    xr_copy = pltpu.make_async_copy(xr_hbm, xr, xsem)
-    xr_copy.start()
     offsets = fetch_blocks(off_hbm, off, p_hbm, pbuf, osem, psem)
 
     def inner(h, carry):
@@ -196,7 +191,6 @@
         fields[t] = after_ref[h] - xr[t - per_plane]
         return carry
 
-    xr_copy.wait()
     lax.fori_loop(per_plane, rows - per_plane, inner, 0, unroll=8)
     lax.fori_loop(0, per_plane, edge, 0, unroll=8)
     offsets.wait()
@@ -310,18 +304,16 @@
     def scratch(fields):
         return [
             pltpu.SMEM((slots,), jnp.int32),
-            pltpu.VMEM((rows, cols, LANES), BF),
             pltpu.VMEM((rows, fields * cols, LANES), BF),
             pltpu.VMEM((slots, proj, win), BF),
             dma,
-            dma,
             dma((slots,)),
         ]
 
     e_yz = pl.pallas_call(
         inside_kernel,
         out_shape=jax.ShapeDtypeStruct((slots, 2 * cols, LANES), BF),
-        in_specs=[hbm] * 3,
+        in_specs=[hbm, vmem, hbm],
         out_specs=vmem,
         scratch_shapes=scratch(2),
         compiler_params=params(LIMIT),
@@ -341,7 +333,7 @@
     e_x = pl.pallas_call(
         across_kernel,
         out_shape=jax.ShapeDtypeStruct((slots, cols, LANES), BF),
-        in_specs=[hbm, hbm, vmem, vmem, hbm],
+        in_specs=[hbm, vmem, vmem, vmem, hbm],
         out_specs=vmem,
         scratch_shapes=scratch(1),
         compiler_params=params(LIMIT),

time: 75 us -> 74.9 us (level)
  no operation moved by 1% of the time
where the time goes in v6:
time: 74.9 us; the launch traced here: 74.5 us
  blocking collectives  30.5 us (41%)
  Pallas kernels  22.2 us (30%)
  starting transfers between devices  16 us (21%)
  waiting for transfers between devices  3.39 us (5%)
  matrix products  0.98 us (1%)
    all_to_all x1, blocking collectives, forces(): gathered = lax.all_to_all(shares, ('band', 'pole'), 0, 0, tiled=True)  20.8 us
    all_to_all x1, blocking collectives, forces(): at_owner = lax.all_to_all(terms, 'grid', 0, 0, tiled=True)  9.69 us
    pallas_call x1, Pallas kernels, forces(): pl.pallas_call(value_kernel, out_shape=(jax.ShapeDtypeStruct((rows, cols,...  7.89 us
    all_to_all x1, starting transfers between devices, forces(): arrived = lax.all_to_all(c_part, 'grid', 0, 0, tiled=True)  7.59 us
    pallas_call x1, Pallas kernels, forces(): pl.pallas_call(across_kernel, out_shape=jax.ShapeDtypeStruct((slots, cols...  6.86 us
    pallas_call x1, Pallas kernels, forces(): pl.pallas_call(inside_kernel, out_shape=jax.ShapeDtypeStruct((slots, 2 *...  5.86 us
    all_to_all x1, starting transfers between devices, forces(): lax.all_to_all(summed.reshape(bricks, slots, per * LANES), 'grid', 0, 0,...  3.53 us
    ppermute x1, starting transfers between devices, forces(): after = lax.ppermute(lo, 'grid', down)  3.5 us
  transfers between devices with their start and end apart: 4, of which 1 were waited for; matrix products, arithmetic and copies ran while one was open for 1% of the time, Pallas kernels for 17%

profile of v6, /device:TPU:1, one launch (start us, length us, event | category | flops | bytes accessed | tf_op | source)
XLA Modules:
  0.0 74.5 jit_solution(1497505440103598936)
XLA Ops:
  0.0 7.9 %values.1 = (bf16[128,64,128]{2,1,0:T(8,128)(2,1)S(1)}, bf16[32,64,128]{2,1,0:T(8,128)(2,1)}, bf16[32,64,128]{2,1,0:T(8,128)(2,1)}, bf16[16,16,512]{2,1,0:T(8,128)(2,1)}) custom-call(s32[16]{0:T(128)} %off_hbm.5, bf16[64,4,16,256]{3,2,1,0:T(8,128)(2,1)} %bitcast.5, bf16[16,128,2048]{2,1,0:T(8,128)(2,1)} %p_hbm.5), custom_call_target="tpu_custom_call" | custom-call | tf_op jit(solution)/shard_map/values/pallas_call | solution.py:271
  7.9 7.6 %all-to-all-start = ((bf16[16,16,512]{2,1,0:T(8,128)(2,1)}), bf16[16,16,512]{2,1,0:T(8,128)(2,1)S(1)}, u32[]{:S(2)}, u32[]{:S(2)}) async-start(bf16[16,16,512]{2,1,0:T(8,128)(2,1)} %get-tuple-element.11), calls=%async_computation | async-start | bytes 524288 | tf_op jit(solution)/shard_map/all_to_all | solution.py:297
  15.5 1.4 %collective-permute-start = (bf16[32,64,128]{2,1,0:T(8,128)(2,1)}, bf16[32,64,128]{2,1,0:T(8,128)(2,1)}, u32[]{:S(2)}, u32[]{:S(2)}) collective-permute-start(bf16[32,64,128]{2,1,0:T(8,128)(2,1)} %get-tuple-element.14), channel_id=1, source_target_pairs={{0,16},{16,32},{32,48},{48,64},{64,80},{80,96},{96,112},{112,128},... | collective-permute-start | bytes 1572872 | tf_op jit(solution)/shard_map/ppermute | solution.py:301
  16.9 3.5 %collective-permute-start.1 = (bf16[32,64,128]{2,1,0:T(8,128)(2,1)}, bf16[32,64,128]{2,1,0:T(8,128)(2,1)}, u32[]{:S(2)}, u32[]{:S(2)}) collective-permute-start(bf16[32,64,128]{2,1,0:T(8,128)(2,1)} %get-tuple-element.15), channel_id=1, source_target_pairs={{16,0},{32,16},{48,32},{64,48},{80,64},{96,80},{112,96},{128,112},... | collective-permute-start | bytes 1572872 | tf_op jit(solution)/shard_map/ppermute | solution.py:302
  20.4 0.0 copy-start
  20.4 5.9 %inside.1.eyz_ref = bf16[16,128,128]{2,1,0:T(8,128)(2,1)S(1)} custom-call(s32[16]{0:T(128)} %off_hbm.5, bf16[128,64,128]{2,1,0:T(8,128)(2,1)S(1)} %get-tuple-element.12.xr, bf16[16,128,2048]{2,1,0:T(8,128)(2,1)} %p_hbm.5), custom_call_target="tpu_custom_call" | custom-call | tf_op jit(solution)/shard_map/inside/pallas_call | solution.py:313
  26.2 0.0 copy-done
  26.2 0.1 eq.15
  26.3 0.0 all-to-all-done
  26.3 1.0 %convolution_convert_fusion = bf16[256,512]{1,0:T(8,128)(2,1)} fusion(bf16[256,512]{1,0:T(8,128)(2,1)S(1)} %bitcast.6, s32[256]{0:T(256)S(1)} %eq.15), kind=kOutput, calls=%fused_computation | convolution fusion | flops 67305472 | bytes 525312 | tf_op jit(solution)/shard_map/dot_general | solution.py:326
  27.3 3.5 %all-to-all-start.1 = ((bf16[16,16,512]{2,1,0:T(8,128)(2,1)}), bf16[16,16,512]{2,1,0:T(8,128)(2,1)S(1)}, u32[]{:S(2)}, u32[]{:S(2)}) async-start(bf16[16,16,512]{2,1,0:T(8,128)(2,1)} %bitcast.3), calls=%async_computation.1 | async-start | bytes 524288 | tf_op jit(solution)/shard_map/all_to_all | solution.py:329
  31.5 0.0 copy-start.1
  31.5 0.0 copy-start.2
  31.5 3.4 %collective-permute-done.before_ref = bf16[32,64,128]{2,1,0:T(8,128)(2,1)} collective-permute-done((bf16[32,64,128]{2,1,0:T(8,128)(2,1)}, bf16[32,64,128]{2,1,0:T(8,128)(2,1)}, u32[]{:S(2)}, u32[]{:S(2)}) %collective-permute-start) | collective-permute-done | bytes 524320 | tf_op jit(solution)/shard_map/ppermute | solution.py:301
  34.9 0.0 collective-permute-done.1.after_ref
  34.9 6.9 %across.1.ex_ref = bf16[16,64,128]{2,1,0:T(8,128)(2,1)S(1)} custom-call(s32[16]{0:T(128)} %off_hbm.5, bf16[128,64,128]{2,1,0:T(8,128)(2,1)S(1)} %get-tuple-element.12.xr, bf16[32,64,128]{2,1,0:T(8,128)(2,1)} %collective-permute-done.before_ref, bf16[32,64,128]{2,1,0:T(8,128)(2,1)} %collective-permute-done.1.after_ref, bf16[16,128,2048]{2,1,0:T(8,128)(2,1)} %p_hbm.5), custom_call_target="tpu_custom_call" | custom-call | tf_op jit(solution)/shard_map/across/pallas_call | solution.py:333
  41.8 0.0 all-to-all-done.1.c_ref
  41.8 1.4 %terms.1 = bf16[16,8,384]{2,1,0:T(8,128)(2,1)S(1)} custom-call(s32[16,16]{1,0:T(8,128)S(1)} %copy-done, s32[1]{0:T(128)} %bitcast.brick_ref, f32[1]{0:T(128)S(6)} %copy.8.w_ref, bf16[16,16,512]{2,1,0:T(8,128)(2,1)S(1)} %all-to-all-done.1.c_ref, bf16[16,64,128]{2,1,0:T(8,128)(2,1)S(1)} %across.1.ex_ref, bf16[16,128,128]{2,1,0:T(8,128)(2,1)S(1)} %inside.1.eyz_ref), custom_call_target="tpu_custom_call" | custom-call | tf_op jit(solution)/shard_map/terms/pallas_call | solution.py:343
  43.1 9.7 %all_to_all.20.t_ref = bf16[16,8,384]{2,1,0:T(8,128)(2,1)S(1)} all-to-all(bf16[16,8,384]{2,1,0:T(8,128)(2,1)S(1)} %terms.1), channel_id=1, replica_groups=mesh['grid'=16,'band'=8,'pole'=2] {'grid'}, dimensions={0} | all-to-all | bytes 196608 | tf_op jit(solution)/shard_map/all_to_all | solution.py:356
  52.8 0.0 copy-done.1
  52.8 0.0 copy-done.2
  52.8 0.2 owner.1
  53.0 20.8 %all_to_all.21 = f32[16,8,128]{2,1,0:T(8,128)S(1)} all-to-all(f32[16,8,128]{2,1,0:T(8,128)S(1)} %owner.1), channel_id=1, replica_groups=mesh['grid'=16,'band'=8,'pole'=2] {'band','pole'}, dimensions={0} | all-to-all | bytes 131072 | tf_op jit(solution)/shard_map/all_to_all | solution.py:364
  73.9 0.6 slice_reduce_fusion
Async XLA Ops:
  7.9 18.4 %all-to-all-start = ((bf16[16,16,512]{2,1,0:T(8,128)(2,1)}), bf16[16,16,512]{2,1,0:T(8,128)(2,1)S(1)}, u32[]{:S(2)}, u32[]{:S(2)}) async-start(bf16[16,16,512]{2,1,0:T(8,128)(2,1)} %get-tuple-element.11), calls=%async_computation | async-start | bytes 524288 | tf_op jit(solution)/shard_map/all_to_all | solution.py:297
  15.5 19.4 %collective-permute-start = (bf16[32,64,128]{2,1,0:T(8,128)(2,1)}, bf16[32,64,128]{2,1,0:T(8,128)(2,1)}, u32[]{:S(2)}, u32[]{:S(2)}) collective-permute-start(bf16[32,64,128]{2,1,0:T(8,128)(2,1)} %get-tuple-element.14), channel_id=1, source_target_pairs={{0,16},{16,32},{32,48},{48,64},{64,80},{80,96},{96,112},{112,128},... | collective-permute-start | bytes 1572872 | tf_op jit(solution)/shard_map/ppermute | solution.py:301
  16.9 18.0 %collective-permute-start.1 = (bf16[32,64,128]{2,1,0:T(8,128)(2,1)}, bf16[32,64,128]{2,1,0:T(8,128)(2,1)}, u32[]{:S(2)}, u32[]{:S(2)}) collective-permute-start(bf16[32,64,128]{2,1,0:T(8,128)(2,1)} %get-tuple-element.15), channel_id=1, source_target_pairs={{16,0},{32,16},{48,32},{64,48},{80,64},{96,80},{112,96},{128,112},... | collective-permute-start | bytes 1572872 | tf_op jit(solution)/shard_map/ppermute | solution.py:302
  20.4 5.9 %copy-start = (s32[16,16]{1,0:T(8,128)S(1)}, s32[16,16]{1,0:T(8,128)}, u32[]{:S(2)}) copy-start(s32[16,16]{1,0:T(8,128)} %blk_ref.1) | copy-start | bytes 3076
  27.3 14.5 %all-to-all-start.1 = ((bf16[16,16,512]{2,1,0:T(8,128)(2,1)}), bf16[16,16,512]{2,1,0:T(8,128)(2,1)S(1)}, u32[]{:S(2)}, u32[]{:S(2)}) async-start(bf16[16,16,512]{2,1,0:T(8,128)(2,1)} %bitcast.3), calls=%async_computation.1 | async-start | bytes 524288 | tf_op jit(solution)/shard_map/all_to_all | solution.py:329
  31.5 21.3 %copy-start.1 = (f32[8,128]{1,0:T(8,128)S(1)}, f32[8,128]{1,0:T(8,128)}, u32[]{:S(2)}) copy-start(f32[8,128]{1,0:T(8,128)} %coef_ref.1) | copy-start | bytes 12292
  31.5 21.3 %copy-start.2 = (s32[8,128]{1,0:T(8,128)S(1)}, s32[8,128]{1,0:T(8,128)}, u32[]{:S(2)}) copy-start(s32[8,128]{1,0:T(8,128)} %atom_ref.1) | copy-start | bytes 12292
